TPU v7x, 256 devices: a whole 4x4x8 slice. The times are simulated.
256 devices in a mesh: member: 2 (over x_lo), space: 128 (over z, y, x_hi, core).
Axes of the slice: x: 4 (x_hi: 2, x_lo: 2; x = x_hi * 2 + x_lo), y: 4, z: 8, core: 2. Of those that a mesh axis runs over, the one named last changes fastest.
Arguments:
- params: float32 [256, 512, 1024], P('member', 'space'), may hold values from -2 to 2
- state: float32 [256, 512, 1024], P('member', 'space'), may hold values from -6 to 6
- regime: int32 [512, 1024], P('space'), may hold values from 0 to 7
- regime_coefs: float32 [8, 4], replicated, may hold values from 0.1 to 0.5
- observation_index: int32 [65536], P('space'), may hold values from 0 to 524287, as said below
- measured_values: float32 [65536], P('space'), may hold values from -6 to 6
- observation_spread: float32 [65536], P('space'), may hold values from 0.1 to 1
- observation_jitter: float32 [256, 65536], P('member', 'space'), may hold values from -6 to 6
Outputs:
- revised_log_diffusivity: float32 [256, 512, 1024], P('member', 'space')
- predicted_member_state: float32 [256, 512, 1024], P('member', 'space')
Inputs may be any that keep to these rules, and one draw needn't show every extreme that they name: `observation_index`: observation o lies in the strip of rows o // 512 * 4 up to (o // 512 + 1) * 4 - 1; the first observation of each strip sits on its first cell, the second on its last cell; cells may repeat.
All inputs are finite; a program needn't handle non-finite values.
Results may differ from a plain program's by a relative error of at most 0.015.
Values sent between devices are 32-bit elements; how exact they have to be, the bound alone decides.
No kernel may reach another device: no remote copies, remote signals or barrier semaphores. Data moves between devices by JAX's collectives and lax.ppermute only.
A program may use at most 64 MiB of HBM per device.

v0:
```python
import math

import jax
import jax.numpy as jnp
from jax import lax
from jax.sharding import PartitionSpec as P

time_step = 0.06


def with_halo(cells, sides, width):
    for axis, dim in sides:
        count = lax.axis_size(axis)
        ends = count - 1
        head = lax.slice_in_dim(cells, 0, width, axis=dim)
        tail = lax.slice_in_dim(cells, cells.shape[dim] - width, cells.shape[dim], axis=dim)
        cells = jnp.concatenate(
            [
                lax.ppermute(tail, axis, [(i, (i + 1) % count) for i in range(ends)]),
                cells,
                lax.ppermute(head, axis, [((i + 1) % count, i) for i in range(ends)]),
            ],
            axis=dim,
        )
    return cells


def coef_fields(regime, regime_coefs):
    levels = jnp.arange(regime_coefs.shape[0], dtype=jnp.int32)
    onehot = (regime[None, :, :] == levels[:, None, None]).astype(jnp.float32)
    return jnp.einsum("rd,rxy->dxy", regime_coefs, onehot, precision=lax.Precision.HIGHEST)


def advance(extended, rates, coefs):
    center = extended[..., 1:-1, :]
    widths = [(0, 0)] * (center.ndim - 1) + [(1, 1)]
    padded_cols = jnp.pad(center, widths)
    above = extended[..., :-2, :]
    below = extended[..., 2:, :]
    left_side = padded_cols[..., :-2]
    right_side = padded_cols[..., 2:]
    flow = coefs[0] * (above - center) + coefs[1] * (below - center)
    flow = flow + coefs[2] * (left_side - center) + coefs[3] * (right_side - center)
    return center + rates * flow


def body(
    params,
    state,
    regime,
    regime_coefs,
    observation_index,
    measured_values,
    observation_spread,
    observation_jitter,
):
    block_members = params.shape[0]
    strip_rows = params.shape[1]
    columns = params.shape[2]
    member_list = block_members * lax.axis_size("member")
    square_root_scale = math.sqrt(member_list - 1)
    coefs = coef_fields(regime, regime_coefs)
    rates = time_step * jnp.exp(params)
    current = state
    for repeat in range(2):
        extended = with_halo(current, (("space", 1),), 1)
        current = advance(extended, rates, coefs)
    param_anom = params / square_root_scale
    slab_local_index = observation_index - lax.axis_index("space") * (strip_rows * columns)
    flattened_grid = current.reshape(block_members, strip_rows * columns)
    local_predictions = jnp.take(flattened_grid, slab_local_index, axis=1)
    predicted_fields, noise_draws = (
        lax.all_gather(local_predictions, "member", axis=0, tiled=True),
        lax.all_gather(observation_jitter, "member", axis=0, tiled=True),
    )
    ensemble_mean_prediction = jnp.sum(predicted_fields, axis=0) / member_list
    member_departures = (predicted_fields - ensemble_mean_prediction[None, :]) / (
        observation_spread[None, :] * square_root_scale
    )
    observation_misfits = (
        measured_values[None, :] + observation_spread[None, :] * noise_draws - predicted_fields
    ) / observation_spread[None, :]
    stacked = jnp.concatenate([member_departures, observation_misfits], axis=0)
    own_start = lax.axis_index("member") * block_members
    own_anoms = lax.dynamic_slice_in_dim(member_departures, own_start, block_members, 0)
    block_rows = jnp.dot(
        own_anoms, stacked.T, precision=lax.Precision.HIGHEST, preferred_element_type=jnp.float32
    )
    block_rows = lax.psum(block_rows, "space")
    gram_full = lax.all_gather(block_rows, "member", axis=0, tiled=True)
    gram = gram_full[:, :member_list]
    cross = gram_full[:, member_list:]
    system = jnp.eye(member_list, dtype=jnp.float32) + gram
    factor = jnp.linalg.cholesky(system)
    mixing = jax.scipy.linalg.cho_solve((factor, True), cross)
    empty = jnp.zeros(params.shape, jnp.float32)
    piece = lax.all_gather(param_anom, "member", axis=0, tiled=True)
    weights = lax.dynamic_slice(mixing, (0, own_start), (piece.shape[0], block_members))
    update = empty + jnp.einsum("kj,kxy->jxy", weights, piece, precision=lax.Precision.HIGHEST)
    revised_log_diffusivity = params + update
    return (revised_log_diffusivity, current)


def solution(mesh):
    in_specs = (
        P("member", "space", None),
        P("member", "space", None),
        P("space", None),
        P(),
        P("space"),
        P("space"),
        P("space"),
        P("member", "space"),
    )
    out_specs = (P("member", "space", None), P("member", "space", None))
    return jax.shard_map(body, mesh=mesh, in_specs=in_specs, out_specs=out_specs, check_vma=False)
```

profile of v0, /device:TPU:2, one launch (start us, length us, event | category | flops | bytes accessed | tf_op | source)
XLA Modules:
  0.0 1354.1 jit_solution(15341635839725576717)
XLA Ops:
  8.1 2.8 copy.28
  10.9 1.3 copy-done.3
  12.2 1.0 fusion.53
  13.2 1.8 collective-permute-start
  15.0 1.3 collective-permute-start.1
  16.7 4.2 collective-permute-done.1
  20.9 5.7 fusion.5
  26.6 1.3 copy-done.2
  28.0 1.1 fusion.52
  29.0 13.7 %collective-permute-start.2 = (f32[128,1,1024]{2,0,1:T(8,128)}, f32[128,1,1024]{2,0,1:T(8,128)}, u32[]{:S(2)}, u32[]{:S(2)}) collective-permute-start(f32[128,1,1024]{2,0,1:T(8,128)} %get-tuple-element.28), channel_id=1, source_target_pairs={{0,1},{1,2},{2,3},{3,4},{4,5},{5,6},{6,7},{7,8},{8,9},{9,10},{10,1... | collective-permute-start | bytes 1572872 | tf_op jit(solution)/shard_map/ppermute | solution.py:19
  42.7 1.3 collective-permute-start.3
  44.2 15.5 %all_gather.13 = f32[256,512]{0,1:T(8,128)S(1)} all-gather(f32[128,512]{0,1:T(8,128)S(1)} %copy.30), channel_id=1, replica_groups=mesh['member'=2,'space'=128] {'member'}, dimensions={0}, use_global_device_ids=true | all-gather | bytes 786432 | tf_op jit(solution)/shard_map/all_gather | solution.py:74
  59.7 7.4 fusion.13
  67.1 2.9 copy.29
  70.0 2.6 gather_fusion
  72.8 9.4 all_gather.12
  82.7 2.5 fusion.26
  85.9 4.3 copy.37
  90.1 1177.8 %all-reduce.5.cloned.1.call-done = f32[128,512]{0,1:T(8,128)} async-done(((f32[128,512]{0,1:T(8,128)}), f32[128,512]{0,1:T(8,128)}) %all-reduce.5.cloned.1.call-update) | async-done | bytes 262160 | tf_op jit(solution)/shard_map/psum | solution.py:89
  1267.9 8.1 all_gather.14
  1276.2 11.7 cholesky.50
  1288.0 9.8 custom-call.18
  1298.3 11.7 cholesky.105
  1310.0 0.6 compare_reduce_fusion
  1310.6 0.6 compare_reduce_fusion.1
  1312.6 4.0 while.1
  1312.8 0.6 fusion.64
  1313.4 1.3 bitcast_dynamic-update-slice_fusion.2
  1315.3 1.3 bitcast_dynamic-update-slice_fusion.2
  1316.6 19.7 %custom-call.19 = f32[2,128,128]{1,2,0:T(8,128)S(1)} custom-call(f32[2,128,128]{2,1,0:T(8,128)S(1)} %get-tuple-element.9), custom_call_target="InvertDiagBlocksLowerTriangular" | custom-call | tf_op jit(solution)/shard_map/jit(_cho_solve)/triangular_solve | solution.py:95
  1338.2 5.7 copy_add_fusion
  1343.9 2.7 copy.36
  (58 shorter events, 5.1 us)
Async XLA Ops:
  8.0 8.3 copy-start
  8.0 1259.9 %all-reduce.5.cloned.1.call-start = ((), (), s32[]{:S(2)}) async-start(), calls=%async_computation | async-start | bytes 524288 | tf_op jit(solution)/shard_map/psum | solution.py:89
  8.1 8.3 copy-start.5
  10.9 1.3 copy-start.3
  12.2 8.7 copy-start.1
  13.2 3.5 collective-permute-start
  15.0 5.9 collective-permute-start.1
  26.6 1.3 copy-start.2
  28.0 16.1 %copy-start.7 = (s32[512]{0:T(512)S(1)}, s32[512]{0:T(512)}, u32[]{:S(2)}) copy-start(s32[512]{0:T(512)} %param.12) | copy-start | bytes 6148
  28.0 16.1 %copy-start.4 = (f32[128,512]{1,0:T(8,128)S(1)}, f32[128,512]{1,0:T(8,128)}, u32[]{:S(2)}) copy-start(f32[128,512]{1,0:T(8,128)} %param.15) | copy-start | bytes 786436
  28.0 31.7 %copy-start.6 = (f32[512]{0:T(512)S(1)}, f32[512]{0:T(512)}, u32[]{:S(2)}) copy-start(f32[512]{0:T(512)} %param.14) | copy-start | bytes 6148
  29.0 30.6 %collective-permute-start.2 = (f32[128,1,1024]{2,0,1:T(8,128)}, f32[128,1,1024]{2,0,1:T(8,128)}, u32[]{:S(2)}, u32[]{:S(2)}) collective-permute-start(f32[128,1,1024]{2,0,1:T(8,128)} %get-tuple-element.28), channel_id=1, source_target_pairs={{0,1},{1,2},{2,3},{3,4},{4,5},{5,6},{6,7},{7,8},{8,9},{9,10},{10,1... | collective-permute-start | bytes 1572872 | tf_op jit(solution)/shard_map/ppermute | solution.py:19
  42.7 16.9 %collective-permute-start.3 = (f32[128,1,1024]{2,0,1:T(8,128)}, f32[128,1,1024]{2,0,1:T(8,128)}, u32[]{:S(2)}, u32[]{:S(2)}) collective-permute-start(f32[128,1,1024]{2,0,1:T(8,128)} %get-tuple-element.29), channel_id=1, source_target_pairs={{1,0},{2,1},{3,2},{4,3},{5,4},{6,5},{7,6},{8,7},{9,8},{10,9},{11,1... | collective-permute-start | bytes 1572872 | tf_op jit(solution)/shard_map/ppermute | solution.py:21
  70.0 12.3 copy-start.8
  85.3 1252.9 %all-gather.2.cloned.1.call-start = ((), (), s32[]{:S(2)}) async-start(), calls=%async_computation.1 | async-start | bytes 6291456 | tf_op jit(solution)/shard_map/all_gather | solution.py:97
Sparse Core Ops, SparseCore 0:
  85.4 1182.4 all-reduce.4
Sparse Core Ops, SparseCore 1:
  87.5 65.5 all-gather.1
where the time goes:
time: 1350 us
  waiting for transfers between devices  1180 us (87%)
  other arithmetic  68.1 us (5%)
  blocking collectives  32.9 us (2%)
  local copies, waits for them, and re-layouts  24.2 us (2%)
  starting transfers between devices  18.1 us (1%)
  between operations  17.1 us (1%)
    psum x1, waiting for transfers between devices, body(): block_rows = lax.psum(block_rows, 'space')  1180 us
    another operation x7, other arithmetic, body(): factor = jnp.linalg.cholesky(system)  34.6 us
  transfers between devices with their start and end apart: 6, of which 3 were waited for; matrix products, arithmetic and copies ran while one was open for 5% of the time, Pallas kernels for 0%

commit v1 on v0

v1 whole, which is shorter than its diff:
```python
import math

import jax
import jax.numpy as jnp
from jax import lax
from jax.sharding import Mesh, PartitionSpec as P

time_step = 0.06
SPACE = ("z", "y", "xh", "core")
CHIPS = ("z", "y", "xh")
SWAP = [(0, 1), (1, 0)]


def coef_fields(regime, regime_coefs):
    levels = jnp.arange(regime_coefs.shape[0], dtype=jnp.int32)
    onehot = (regime[None, :, :] == levels[:, None, None]).astype(jnp.float32)
    return jnp.einsum("rd,rxy->dxy", regime_coefs, onehot, precision=lax.Precision.HIGHEST)


def with_halo(cells):
    count = lax.axis_size(SPACE)
    ends = count - 1
    head = cells[:, :1]
    tail = cells[:, -1:]
    above = lax.ppermute(tail, SPACE, [(i, i + 1) for i in range(ends)])
    below = lax.ppermute(head, SPACE, [(i + 1, i) for i in range(ends)])
    return jnp.concatenate([above, cells, below], axis=1)


def advance(extended, rates, coefs):
    center = extended[..., 1:-1, :]
    widths = [(0, 0)] * (center.ndim - 1) + [(1, 1)]
    padded_cols = jnp.pad(center, widths)
    above = extended[..., :-2, :]
    below = extended[..., 2:, :]
    left_side = padded_cols[..., :-2]
    right_side = padded_cols[..., 2:]
    flow = coefs[0] * (above - center) + coefs[1] * (below - center)
    flow = flow + coefs[2] * (left_side - center) + coefs[3] * (right_side - center)
    return center + rates * flow


def reduce_over_space(block):
    half = block.shape[0] // 2
    core = lax.axis_index("core")
    low, high = block[:half], block[half:]
    first = core == 0
    kept = jnp.where(first, low, high)
    sent = jnp.where(first, high, low)
    part = kept + lax.ppermute(sent, "core", SWAP)
    chips = lax.axis_size(CHIPS)
    pieces = lax.all_to_all(part, CHIPS, 0, 0, tiled=True)
    piece = jnp.sum(pieces.reshape(chips, half // chips, -1), axis=0)
    spread = jnp.broadcast_to(piece[None], (chips,) + piece.shape).reshape(half, -1)
    summed = lax.all_to_all(spread, CHIPS, 0, 0, tiled=True)
    other = lax.ppermute(summed, "core", SWAP)
    return jnp.concatenate(
        [jnp.where(first, summed, other), jnp.where(first, other, summed)], axis=0
    )


def body(
    params,
    state,
    regime,
    regime_coefs,
    observation_index,
    measured_values,
    observation_spread,
    observation_jitter,
):
    own = params.shape[0]
    strip_rows = params.shape[1]
    columns = params.shape[2]
    members = own * lax.axis_size("member")
    square_root_scale = math.sqrt(members - 1)
    coefs = coef_fields(regime, regime_coefs)
    rates = time_step * jnp.exp(params)
    current = state
    for repeat in range(2):
        current = advance(with_halo(current), rates, coefs)
    local_index = observation_index - lax.axis_index(SPACE) * (strip_rows * columns)
    flat = current.reshape(own, strip_rows * columns)
    mine = jnp.take(flat, local_index, axis=1)
    theirs = lax.ppermute(mine, "member", SWAP)
    params_there, theirs2 = lax.optimization_barrier((params, theirs))
    other_params = lax.ppermute(params_there, "member", SWAP)
    predicted = jnp.concatenate([mine, theirs2], axis=0)
    mean = jnp.sum(predicted, axis=0) / members
    anomalies = (predicted - mean[None, :]) / (observation_spread[None, :] * square_root_scale)
    innovations = (
        measured_values[None, :] + observation_spread[None, :] * observation_jitter - mine
    ) / observation_spread[None, :]
    stacked = jnp.concatenate([anomalies, innovations], axis=0)
    rows = jnp.dot(
        anomalies, stacked.T, precision=lax.Precision.HIGHEST, preferred_element_type=jnp.float32
    )
    total = reduce_over_space(rows)
    gram = total[:, :members]
    cross = total[:, members:]
    system = jnp.eye(members, dtype=jnp.float32) + gram
    factor = jnp.linalg.cholesky(system)
    mixing = jax.scipy.linalg.cho_solve((factor, True), cross)
    both = jnp.concatenate([params, other_params], axis=0) / square_root_scale
    update = jnp.einsum("kj,kxy->jxy", mixing, both, precision=lax.Precision.HIGHEST)
    return (params + update, current)


def solution(mesh):
    fine = Mesh(mesh.devices.reshape(2, 8, 4, 2, 2), ("member",) + SPACE)
    in_specs = (
        P("member", SPACE, None),
        P("member", SPACE, None),
        P(SPACE, None),
        P(),
        P(SPACE),
        P(SPACE),
        P(SPACE),
        P("member", SPACE),
    )
    out_specs = (P("member", SPACE, None), P("member", SPACE, None))
    return jax.shard_map(body, mesh=fine, in_specs=in_specs, out_specs=out_specs, check_vma=False)
```

time: 1350 us -> 194 us (0.14)
  waiting for transfers between devices: 1180 us -> 13.4 us
  blocking collectives: 32.9 us -> 49 us
  between operations: 17.1 us -> 2.4 us
    psum x1 -> x0, waiting for transfers between devices: 1180 us -> none  [body(): block_rows = lax.psum(block_rows, 'space')]
    all_to_all x0 -> x2, blocking collectives: none -> 49 us  [the longest x1 31.4 us: reduce_over_space(): pieces = lax.all_to_all(part, CHIPS, 0, 0, tiled=True)]
    all_gather x3 -> x0, blocking collectives: 32.9 us -> none  [the longest x1 15.5 us: body(): lax.all_gather(observation_jitter, 'member', axis=0, tiled=True)]
    ppermute x4 -> x8, starting transfers between devices: 18 us -> 28.3 us  [the longest x2 14.8 us: with_halo(): above = lax.ppermute(tail, SPACE, [(i, i + 1) for i in range(ends)])]
  transfers between devices with their start and end apart: 6 -> 8, of which waited for: 3 -> 5; matrix products, arithmetic and copies ran while one was open for 5% -> 36% of each run, Pallas kernels for 0% -> 0%
where the time goes in v1:
time: 194 us; the launch traced here: 192 us
  other arithmetic  65.4 us (34%)
  blocking collectives  49 us (25%)
  starting transfers between devices  28.3 us (15%)
  local copies, waits for them, and re-layouts  25.2 us (13%)
  waiting for transfers between devices  13.4 us (7%)
  matrix products  7.89 us (4%)
  between operations  2.4 us (1%)
    another operation x7, other arithmetic, body(): factor = jnp.linalg.cholesky(system)  34.7 us
    all_to_all x1, blocking collectives, reduce_over_space(): pieces = lax.all_to_all(part, CHIPS, 0, 0, tiled=True)  31.4 us
    another operation x3, other arithmetic, body(): mixing = jax.scipy.linalg.cho_solve((factor, True), cross)  19.7 us
    all_to_all x1, blocking collectives, reduce_over_space(): summed = lax.all_to_all(spread, CHIPS, 0, 0, tiled=True)  17.6 us
    ppermute x2, starting transfers between devices, with_halo(): above = lax.ppermute(tail, SPACE, [(i, i + 1) for i in range(ends)])  14.8 us
    unnamed x24, local copies, waits for them, and re-layouts  11.2 us
    add x2, other arithmetic, advance(): return center + rates * flow  9.89 us
    ppermute x1, starting transfers between devices, reduce_over_space(): part = kept + lax.ppermute(sent, 'core', SWAP)  9.1 us
  transfers between devices with their start and end apart: 8, of which 5 were waited for; matrix products, arithmetic and copies ran while one was open for 36% of the time, Pallas kernels for 0%

profile of v1, /device:TPU:2, one launch (start us, length us, event | category | flops | bytes accessed | tf_op | source)
XLA Modules:
  0.0 191.7 jit_solution(3517962931061941460)
XLA Ops:
  0.7 2.8 %copy.44 = f32[128,4,1024]{2,0,1:T(8,128)S(1)} copy(f32[128,4,1024]{2,1,0:T(4,128)} %param.9) | data formatting | bytes 4194304 | tf_op args[1]
  3.6 1.9 collective-permute-start
  5.5 1.3 collective-permute-start.1
  7.1 4.1 %collective-permute-done.1 = f32[128,1,1024]{2,0,1:T(8,128)S(1)} collective-permute-done((f32[128,1,1024]{2,0,1:T(8,128)S(1)}, f32[128,1,1024]{2,0,1:T(8,128)S(1)}, u32[]{:S(2)}, u32[]{:S(2)}) %collective-permute-start.1) | collective-permute-done | bytes 524320 | tf_op jit(solution)/shard_map/ppermute | solution.py:26
  11.2 2.6 %fusion.8 = f32[128,4,1024]{2,0,1:T(8,128)S(1)} fusion(f32[128,4,1024]{2,0,1:T(8,128)S(1)} %copy.44, f32[128,1,1024]{2,0,1:T(8,128)S(1)} %collective-permute-done.1, f32[128,1,1024]{2,0,1:T(8,128)S(1)} %collective-permute-done, f32[4,1024]{1,0:T(4,128)S(1)} %get-tuple-element.52, f32[4,1024]{1,0:T(4,128)S(1)} %get-tuple-element.53, ...), kind=kLoop, calls=%fused_computation.16 | loop fusion | flops 8388608 | bytes 7405568 | tf_op jit(solution)/shard_map/add | solution.py:40
  13.8 1.3 copy-done.3
  15.1 1.0 fusion.57
  16.1 12.9 %collective-permute-start.2 = (f32[128,1,1024]{2,0,1:T(8,128)}, f32[128,1,1024]{2,0,1:T(8,128)S(1)}, u32[]{:S(2)}, u32[]{:S(2)}) collective-permute-start(f32[128,1,1024]{2,0,1:T(8,128)} %get-tuple-element.36), channel_id=1, source_target_pairs={{0,1},{1,2},{2,3},{3,4},{4,5},{5,6},{6,7},{7,8},{8,9},{9,10},{10,1... | collective-permute-start | bytes 1572872 | tf_op jit(solution)/shard_map/ppermute | solution.py:25
  29.1 1.3 collective-permute-start.3
  30.8 2.5 %collective-permute-done.3 = f32[128,1,1024]{2,0,1:T(8,128)} collective-permute-done((f32[128,1,1024]{2,0,1:T(8,128)}, f32[128,1,1024]{2,0,1:T(8,128)}, u32[]{:S(2)}, u32[]{:S(2)}) %collective-permute-start.3) | collective-permute-done | bytes 524320 | tf_op jit(solution)/shard_map/ppermute | solution.py:26
  33.2 7.3 %fusion.16 = (f32[128,4,1024]{2,0,1:T(8,128)}, f32[128,4,1024]{2,0,1:T(8,128)}) fusion(f32[128,4,1024]{2,0,1:T(8,128)} %copy-done.3, f32[128,1,1024]{2,0,1:T(8,128)} %collective-permute-done.3, f32[128,1,1024]{2,0,1:T(8,128)S(1)} %collective-permute-done.2, f32[4,1024]{1,0:T(4,128)S(1)} %get-tuple-element.52, f32[4,1024]{1,0:T(4,128)S(1)} %get-tuple-element.53, ...), kind=kLoop, calls=%fused_computation.24 | loop fusion | flops 8388608 | bytes 9502720 | tf_op jit(solution)/shard_map/add | solution.py:40
  40.5 2.9 %copy.45 = f32[128,4,1024]{0,2,1:T(8,128)} copy(f32[128,4,1024]{2,0,1:T(8,128)} %get-tuple-element.34) | data formatting | bytes 4194304 | tf_op jit(solution)/shard_map/add | solution.py:40
  43.4 2.6 %gather_fusion = f32[512,128]{1,0:T(8,128)S(1)} fusion(f32[128,4096]{0,1:T(8,128)} %bitcast.56, s32[1024]{0:T(1024)S(1)} %pad_clamp_fusion), kind=kCustom, calls=%fused_computation | custom fusion | bytes 526336 | tf_op jit(solution)/shard_map/jit(_take)/gather | solution.py:84
  47.2 5.6 %collective-permute-done.4 = f32[128,512]{0,1:T(8,128)S(1)} collective-permute-done((f32[128,512]{0,1:T(8,128)S(1)}, f32[128,512]{0,1:T(8,128)S(1)}, u32[]{:S(2)}, u32[]{:S(2)}) %collective-permute-start.4) | collective-permute-done | bytes 262176 | tf_op jit(solution)/shard_map/ppermute | solution.py:85
  53.2 1.4 fusion.31
  54.7 9.1 %collective-permute-start.5 = (f32[128,384]{0,1:T(8,128)S(1)}, f32[128,384]{0,1:T(8,128)S(1)}, u32[]{:S(2)}, u32[]{:S(2)}) collective-permute-start(f32[128,384]{0,1:T(8,128)S(1)} %slice_select_fusion), channel_id=1, source_target_pairs={{0,1},{1,0},{2,3},{3,2},{4,5},{5,4},{6,7},{7,6},{8,9},{9,8},{10,11... | collective-permute-start | bytes 589832 | tf_op jit(solution)/shard_map/ppermute | solution.py:50
  63.8 1.1 collective-permute-done.5
  65.1 31.4 %all_to_all.18 = f32[64,2,384]{2,1,0:T(2,128)S(1)} all-to-all(f32[64,2,384]{2,1,0:T(2,128)S(1)} %all_to_all.12), channel_id=1, replica_groups=mesh['member'=2,'z'=8,'y'=4,'xh'=2,'core'=2] {'z','y','xh'}, dimensions={0} | all-to-all | bytes 393216 | tf_op jit(solution)/shard_map/all_to_all | solution.py:52
  96.7 17.6 %all_to_all.19 = f32[64,2,384]{2,1,0:T(2,128)S(1)} all-to-all(f32[64,2,384]{2,1,0:T(2,128)S(1)} %broadcast_in_dim.30), channel_id=1, replica_groups=mesh['member'=2,'z'=8,'y'=4,'xh'=2,'core'=2] {'z','y','xh'}, dimensions={0} | all-to-all | bytes 393216 | tf_op jit(solution)/shard_map/all_to_all | solution.py:55
  114.8 4.3 %copy.60 = f32[128,4,1024]{2,1,0:T(4,128)} copy(f32[128,4,1024]{2,0,1:T(8,128)} %get-tuple-element.34) | data formatting | bytes 4194304
  119.1 2.5 %copy.55 = f32[128,4,1024]{2,0,1:T(8,128)} copy(f32[128,4,1024]{2,1,0:T(4,128)S(1)} %copy-done.1) | data formatting | bytes 4194304 | tf_op jit(solution)/shard_map/optimization_barrier | solution.py:86
  121.6 0.9 collective-permute-start.7
  122.8 11.7 %cholesky.50 = f32[128,128]{1,0:T(8,128)S(1)} custom-call(f32[128,128]{1,0:T(8,128)S(1)} %cholesky.118), custom_call_target="Cholesky" | custom-call | tf_op jit(solution)/shard_map/jit(cholesky)/cholesky | solution.py:102
  134.6 9.8 %custom-call.18 = f32[1,128,128]{1,2,0:T(8,128)S(1)} custom-call(f32[1,128,128]{2,1,0:T(8,128)S(1)} %get-tuple-element.45), custom_call_target="InvertDiagBlocksLowerTriangular" | custom-call | tf_op jit(solution)/shard_map/jit(cholesky)/cholesky | solution.py:102
  144.9 11.7 %cholesky.105 = f32[128,128]{1,0:T(8,128)S(1)} custom-call(f32[128,128]{1,0:T(8,128)S(1)} %convolution_subtract_fusion.1), custom_call_target="Cholesky" | custom-call | tf_op jit(solution)/shard_map/jit(cholesky)/cholesky | solution.py:102
  156.6 0.7 compare_reduce_fusion
  159.4 4.1 %while.1 = (s32[]{:T(128)}, f32[256,256]{1,0:T(8,128)S(1)}, s32[2,2]{1,0:T(2,128)S(1)}, f32[2,128,128]{2,1,0:T(8,128)S(1)}, s32[]{:T(128)}) while((s32[]{:T(128)}, f32[256,256]{1,0:T(8,128)S(1)}, s32[2,2]{1,0:T(2,128)S(1)}, f32[2,128,128]{2,1,0:T(8,128)S(1)}, s32[]{:T(128)}) %tuple.42), condition=%wide.while_cond, body=%wide.while_body.sunk | while | flops 2 | bytes 131181 | solution.py:103
  160.2 1.4 bitcast_dynamic-update-slice_fusion.2
  162.1 1.4 bitcast_dynamic-update-slice_fusion.2
  163.5 19.7 %custom-call.19 = f32[2,128,128]{1,2,0:T(8,128)S(1)} custom-call(f32[2,128,128]{2,1,0:T(8,128)S(1)} %get-tuple-element.13), custom_call_target="InvertDiagBlocksLowerTriangular" | custom-call | tf_op jit(solution)/shard_map/jit(_cho_solve)/triangular_solve | solution.py:103
  184.8 4.2 %fusion.30 = f32[128,4,1024]{2,0,1:T(8,128)S(1)} fusion(f32[128,4,1024]{2,0,1:T(8,128)S(1)} %copy-done.2, f32[128,4,1024]{2,0,1:T(8,128)} %collective-permute-done.7, f32[128,128]{1,0:T(8,128)S(1)} %fusion.48, f32[128,128]{1,0:T(8,128)S(1)} %fusion.47), kind=kOutput, calls=%fused_computation.43 | convolution fusion | flops 1613266944 | bytes 6422528 | tf_op jit(solution)/shard_map/kj,kxy->jxy/dot_general | solution.py:105
  189.1 2.7 %copy.59 = f32[128,4,1024]{2,1,0:T(4,128)} copy(f32[128,4,1024]{2,0,1:T(8,128)S(1)} %fusion.30) | data formatting | bytes 4194304
  (70 shorter events, 7.5 us)
Async XLA Ops:
  0.6 6.2 %copy-start = (f32[8,4]{0,1:T(4,128)S(1)}, f32[8,4]{0,1:T(4,128)}, u32[]{:S(2)}) copy-start(f32[8,4]{0,1:T(4,128)} %param.11) | copy-start | bytes 388
  0.6 6.2 %copy-start.5 = (s32[4,1024]{1,0:T(4,128)S(1)}, s32[4,1024]{1,0:T(4,128)}, u32[]{:S(2)}) copy-start(s32[4,1024]{1,0:T(4,128)} %param.10) | copy-start | bytes 49156
  3.5 7.7 %copy-start.1 = (f32[128,4,1024]{2,1,0:T(4,128)S(1)}, f32[128,4,1024]{2,1,0:T(4,128)}, u32[]{:S(2)}) copy-start(f32[128,4,1024]{2,1,0:T(4,128)} %param.8) | copy-start | bytes 6291460
  3.6 3.5 %collective-permute-start = (f32[128,1,1024]{2,0,1:T(8,128)S(1)}, f32[128,1,1024]{2,0,1:T(8,128)S(1)}, u32[]{:S(2)}, u32[]{:S(2)}) collective-permute-start(f32[128,1,1024]{2,0,1:T(8,128)S(1)} %get-tuple-element.38), channel_id=1, source_target_pairs={{0,1},{1,2},{2,3},{3,4},{4,5},{5,6},{6,7},{7,8},{8,9},{9,10},{10,1... | collective-permute-start | bytes 1572872 | tf_op jit(solution)/shard_map/ppermute | solution.py:25
  5.5 5.7 %collective-permute-start.1 = (f32[128,1,1024]{2,0,1:T(8,128)S(1)}, f32[128,1,1024]{2,0,1:T(8,128)S(1)}, u32[]{:S(2)}, u32[]{:S(2)}) collective-permute-start(f32[128,1,1024]{2,0,1:T(8,128)S(1)} %get-tuple-element.39), channel_id=1, source_target_pairs={{1,0},{2,1},{3,2},{4,3},{5,4},{6,5},{7,6},{8,7},{9,8},{10,9},{11,1... | collective-permute-start | bytes 1572872 | tf_op jit(solution)/shard_map/ppermute | solution.py:26
  13.8 1.3 copy-start.3
  15.1 15.3 %copy-start.4 = (f32[128,512]{1,0:T(8,128)S(1)}, f32[128,512]{1,0:T(8,128)}, u32[]{:S(2)}) copy-start(f32[128,512]{1,0:T(8,128)} %param.15) | copy-start | bytes 786436
  15.1 15.4 %copy-start.8 = (s32[512]{0:T(512)S(1)}, s32[512]{0:T(512)}, u32[]{:S(2)}) copy-start(s32[512]{0:T(512)} %param.12) | copy-start | bytes 6148
  16.1 14.6 %collective-permute-start.2 = (f32[128,1,1024]{2,0,1:T(8,128)}, f32[128,1,1024]{2,0,1:T(8,128)S(1)}, u32[]{:S(2)}, u32[]{:S(2)}) collective-permute-start(f32[128,1,1024]{2,0,1:T(8,128)} %get-tuple-element.36), channel_id=1, source_target_pairs={{0,1},{1,2},{2,3},{3,4},{4,5},{5,6},{6,7},{7,8},{8,9},{9,10},{10,1... | collective-permute-start | bytes 1572872 | tf_op jit(solution)/shard_map/ppermute | solution.py:25
  29.1 4.1 %collective-permute-start.3 = (f32[128,1,1024]{2,0,1:T(8,128)}, f32[128,1,1024]{2,0,1:T(8,128)}, u32[]{:S(2)}, u32[]{:S(2)}) collective-permute-start(f32[128,1,1024]{2,0,1:T(8,128)} %get-tuple-element.37), channel_id=1, source_target_pairs={{1,0},{2,1},{3,2},{4,3},{5,4},{6,5},{7,6},{8,7},{9,8},{10,9},{11,1... | collective-permute-start | bytes 1572872 | tf_op jit(solution)/shard_map/ppermute | solution.py:26
  43.4 2.7 %copy-start.6 = (f32[512]{0:T(512)S(1)}, f32[512]{0:T(512)}, u32[]{:S(2)}) copy-start(f32[512]{0:T(512)} %param.14) | copy-start | bytes 6148
  43.4 2.7 %copy-start.7 = (f32[512]{0:T(512)S(1)}, f32[512]{0:T(512)}, u32[]{:S(2)}) copy-start(f32[512]{0:T(512)} %param.13) | copy-start | bytes 6148
  46.4 6.5 %collective-permute-start.4 = (f32[128,512]{0,1:T(8,128)S(1)}, f32[128,512]{0,1:T(8,128)S(1)}, u32[]{:S(2)}, u32[]{:S(2)}) collective-permute-start(f32[128,512]{0,1:T(8,128)S(1)} %get-tuple-element.29), channel_id=1, source_target_pairs={{0,128},{128,0},{1,129},{129,1},{2,130},{130,2},{3,131},{131,3},{4... | collective-permute-start | bytes 786440 | tf_op jit(solution)/shard_map/ppermute | solution.py:85
  54.7 10.2 %collective-permute-start.5 = (f32[128,384]{0,1:T(8,128)S(1)}, f32[128,384]{0,1:T(8,128)S(1)}, u32[]{:S(2)}, u32[]{:S(2)}) collective-permute-start(f32[128,384]{0,1:T(8,128)S(1)} %slice_select_fusion), channel_id=1, source_target_pairs={{0,1},{1,0},{2,3},{3,2},{4,5},{5,4},{6,7},{7,6},{8,9},{9,8},{10,11... | collective-permute-start | bytes 589832 | tf_op jit(solution)/shard_map/ppermute | solution.py:50
  114.5 8.0 %collective-permute-start.6 = (f32[128,384]{0,1:T(8,128)S(1)}, f32[128,384]{0,1:T(8,128)S(1)}, u32[]{:S(2)}, u32[]{:S(2)}) collective-permute-start(f32[128,384]{0,1:T(8,128)S(1)} %copy.51), channel_id=1, source_target_pairs={{0,1},{1,0},{2,3},{3,2},{4,5},{5,4},{6,7},{7,6},{8,9},{9,8},{10,11... | collective-permute-start | bytes 589832 | tf_op jit(solution)/shard_map/ppermute | solution.py:56
  121.6 63.2 %collective-permute-start.7 = (f32[128,4,1024]{2,0,1:T(8,128)}, f32[128,4,1024]{2,0,1:T(8,128)}, u32[]{:S(2)}, u32[]{:S(2)}) collective-permute-start(f32[128,4,1024]{2,0,1:T(8,128)} %copy.55), channel_id=1, source_target_pairs={{0,128},{128,0},{1,129},{129,1},{2,130},{130,2},{3,131},{131,3},{4... | collective-permute-start | bytes 6291464 | tf_op jit(solution)/shard_map/ppermute | solution.py:87
  122.8 62.0 %copy-start.2 = (f32[128,4,1024]{2,0,1:T(8,128)S(1)}, f32[128,4,1024]{2,0,1:T(8,128)}, u32[]{:S(2)}) copy-start(f32[128,4,1024]{2,0,1:T(8,128)} %get-tuple-element.35) | copy-start | bytes 6291460

commit v2 on v1

--- a/solution.py
+++ b/solution.py
@@ -3,12 +3,88 @@
 import jax
 import jax.numpy as jnp
 from jax import lax
+from jax.experimental import pallas as pl
+from jax.experimental.pallas import tpu as pltpu
 from jax.sharding import Mesh, PartitionSpec as P
 
 time_step = 0.06
 SPACE = ("z", "y", "xh", "core")
 CHIPS = ("z", "y", "xh")
 SWAP = [(0, 1), (1, 0)]
+HIGHEST = lax.Precision.HIGHEST
+BLOCK = 64
+
+
+def invert_block(block):
+    size = block.shape[0]
+    wide = 2 * size
+    row_id = lax.broadcasted_iota(jnp.int32, (size, wide), 0)
+    r = lax.broadcasted_iota(jnp.int32, (size, size), 0)
+    c = lax.broadcasted_iota(jnp.int32, (size, size), 1)
+    aug = jnp.concatenate([block, (r == c).astype(jnp.float32)], axis=1)
+    for p in range(0, size, 4):
+        cols = [jnp.broadcast_to(aug[:, p + i : p + i + 1], (size, wide)) for i in range(4)]
+        rows = [aug[p + i : p + i + 1, :] for i in range(4)]
+        e = [[cols[j][p + i : p + i + 1, :] for j in range(4)] for i in range(4)]
+        a, b, d = e[0][0], e[1][0], e[1][1]
+        inv = 1.0 / (a * d - b * b)
+        t0 = (d * rows[0] - b * rows[1]) * inv
+        t1 = (a * rows[1] - b * rows[0]) * inv
+        u, v, w, x = e[2][0], e[2][1], e[3][0], e[3][1]
+        l00 = (d * u - b * v) * inv
+        l01 = (a * v - b * u) * inv
+        l10 = (d * w - b * x) * inv
+        l11 = (a * x - b * w) * inv
+        sa = e[2][2] - (u * l00 + v * l01)
+        sb = e[3][2] - (w * l00 + x * l01)
+        sd = e[3][3] - (w * l10 + x * l11)
+        s2 = rows[2] - (l00 * rows[0] + l01 * rows[1])
+        s3 = rows[3] - (l10 * rows[0] + l11 * rows[1])
+        sinv = 1.0 / (sa * sd - sb * sb)
+        n2 = (sd * s2 - sb * s3) * sinv
+        n3 = (sa * s3 - sb * s2) * sinv
+        news = [t0 - (l00 * n2 + l10 * n3), t1 - (l01 * n2 + l11 * n3), n2, n3]
+        out = aug
+        for i in range(4):
+            out = out - cols[i] * news[i]
+        for i in range(4):
+            out = jnp.where(row_id == p + i, news[i], out)
+        aug = out
+    return aug[:, size:]
+
+
+def solve_kernel(g_ref, x_ref, w):
+    m = g_ref.shape[0]
+    w[...] = g_ref[...]
+    r = lax.broadcasted_iota(jnp.int32, (m, m), 0)
+    c = lax.broadcasted_iota(jnp.int32, (m, m), 1)
+    w[:, :m] = w[:, :m] + (r == c).astype(jnp.float32)
+    rows = lax.broadcasted_iota(jnp.int32, (m, 1), 0)
+    for at in range(0, m, BLOCK):
+        end = at + BLOCK
+        lo = end // 128 * 128
+        inv = invert_block(w[at:end, at:end])
+        new = jnp.dot(inv, w[at:end, lo:], precision=HIGHEST, preferred_element_type=jnp.float32)
+        left = jnp.where((rows >= at) & (rows < end), 0.0, w[:, at:end])
+        w[:, lo:] = w[:, lo:] - jnp.dot(
+            left, new, precision=HIGHEST, preferred_element_type=jnp.float32
+        )
+        w[at:end, lo:] = new
+    x_ref[...] = w[:, m:]
+
+
+def solve(system):
+    m, wide = system.shape
+    vmem = pl.BlockSpec(memory_space=pltpu.VMEM)
+    return pl.pallas_call(
+        solve_kernel,
+        out_shape=jax.ShapeDtypeStruct((m, wide - m), jnp.float32),
+        in_specs=[vmem],
+        out_specs=vmem,
+        scratch_shapes=[pltpu.VMEM((m, wide), jnp.float32)],
+        cost_estimate=pl.CostEstimate(flops=200_000_000, bytes_accessed=600_000, transcendentals=0),
+        name="solve",
+    )(system)
 
 
 def coef_fields(regime, regime_coefs):
@@ -59,7 +135,7 @@
     )
 
 
-def body(
+def strip(
     params,
     state,
     regime,
@@ -77,7 +153,7 @@
     coefs = coef_fields(regime, regime_coefs)
     rates = time_step * jnp.exp(params)
     current = state
-    for repeat in range(2):
+    for _ in range(2):
         current = advance(with_halo(current), rates, coefs)
     local_index = observation_index - lax.axis_index(SPACE) * (strip_rows * columns)
     flat = current.reshape(own, strip_rows * columns)
@@ -93,14 +169,9 @@
     ) / observation_spread[None, :]
     stacked = jnp.concatenate([anomalies, innovations], axis=0)
     rows = jnp.dot(
-        anomalies, stacked.T, precision=lax.Precision.HIGHEST, preferred_element_type=jnp.float32
+        anomalies, stacked.T, precision=HIGHEST, preferred_element_type=jnp.float32
     )
-    total = reduce_over_space(rows)
-    gram = total[:, :members]
-    cross = total[:, members:]
-    system = jnp.eye(members, dtype=jnp.float32) + gram
-    factor = jnp.linalg.cholesky(system)
-    mixing = jax.scipy.linalg.cho_solve((factor, True), cross)
+    mixing = solve(reduce_over_space(rows))
     both = jnp.concatenate([params, other_params], axis=0) / square_root_scale
     update = jnp.einsum("kj,kxy->jxy", mixing, both, precision=lax.Precision.HIGHEST)
     return (params + update, current)
@@ -119,4 +190,4 @@
         P("member", SPACE),
     )
     out_specs = (P("member", SPACE, None), P("member", SPACE, None))
-    return jax.shard_map(body, mesh=fine, in_specs=in_specs, out_specs=out_specs, check_vma=False)
+    return jax.shard_map(strip, mesh=fine, in_specs=in_specs, out_specs=out_specs, check_vma=False)

time: 194 us -> 172 us (0.89)
  other arithmetic: 65.4 us -> 11.7 us
  blocking collectives: 49 us -> 72.8 us
  Pallas kernels: 0 us -> 13.7 us
  local copies, waits for them, and re-layouts: 25.2 us -> 19.3 us
  starting transfers between devices: 28.3 us -> 31.6 us
  matrix products: 7.89 us -> 5.6 us
    another operation x10 -> x0, other arithmetic: 54.4 us -> none  [the longest x7 34.7 us: body(): factor = jnp.linalg.cholesky(system)]
    all_to_all x1, blocking collectives: 31.4 us -> 47.2 us  [reduce_over_space(): pieces = lax.all_to_all(part, CHIPS, 0, 0, tiled=True)]
    pallas_call x0 -> x1, Pallas kernels: none -> 13.7 us  [solve(): pl.pallas_call(solve_kernel, out_shape=jax.ShapeDtypeStruct((m, wide - m)...]
    all_to_all x1, blocking collectives: 17.6 us -> 25.6 us  [reduce_over_space(): summed = lax.all_to_all(spread, CHIPS, 0, 0, tiled=True)]
    another operation x9 -> x0, local copies, waits for them, and re-layouts: 4.02 us -> none
    ppermute x1, starting transfers between devices: 9.1 us -> 12.9 us  [reduce_over_space(): part = kept + lax.ppermute(sent, 'core', SWAP)]
    another operation x8 -> x0, matrix products: 2.02 us -> none  [the longest x6 1.55 us: body(): mixing = jax.scipy.linalg.cho_solve((factor, True), cross)]
    unnamed x24 -> x26, local copies, waits for them, and re-layouts: 11.2 us -> 9.66 us
  transfers between devices with their start and end apart: 8 -> 8, of which waited for: 5 -> 5; matrix products, arithmetic and copies ran while one was open for 36% -> 3% of each run, Pallas kernels for 0% -> 8%
where the time goes in v2:
time: 172 us; the launch traced here: 169 us
  blocking collectives  72.8 us (42%)
  starting transfers between devices  31.6 us (18%)
  local copies, waits for them, and re-layouts  19.3 us (11%)
  Pallas kernels  13.7 us (8%)
  waiting for transfers between devices  13.4 us (8%)
  other arithmetic  11.7 us (7%)
  matrix products  5.6 us (3%)
    all_to_all x1, blocking collectives, reduce_over_space(): pieces = lax.all_to_all(part, CHIPS, 0, 0, tiled=True)  47.2 us
    all_to_all x1, blocking collectives, reduce_over_space(): summed = lax.all_to_all(spread, CHIPS, 0, 0, tiled=True)  25.6 us
    ppermute x2, starting transfers between devices, with_halo(): above = lax.ppermute(tail, SPACE, [(i, i + 1) for i in range(ends)])  14.8 us
    pallas_call x1, Pallas kernels, solve(): pl.pallas_call(solve_kernel, out_shape=jax.ShapeDtypeStruct((m, wide - m)...  13.7 us
    ppermute x1, starting transfers between devices, reduce_over_space(): part = kept + lax.ppermute(sent, 'core', SWAP)  12.9 us
    add x2, other arithmetic, advance(): return center + rates * flow  9.88 us
    unnamed x26, local copies, waits for them, and re-layouts  9.66 us
    ppermute x2, waiting for transfers between devices, with_halo(): below = lax.ppermute(head, SPACE, [(i + 1, i) for i in range(ends)])  6.51 us
  transfers between devices with their start and end apart: 8, of which 5 were waited for; matrix products, arithmetic and copies ran while one was open for 3% of the time, Pallas kernels for 8%

profile of v2, /device:TPU:2, one launch (start us, length us, event | category | flops | bytes accessed | tf_op | source)
XLA Modules:
  0.0 169.0 jit_solution(4849511910906634429)
XLA Ops:
  0.7 2.8 %copy.27 = f32[128,4,1024]{2,0,1:T(8,128)S(1)} copy(f32[128,4,1024]{2,1,0:T(4,128)} %param.9) | data formatting | bytes 4194304 | tf_op args[1]
  3.6 1.9 %collective-permute-start = (f32[128,1,1024]{2,0,1:T(8,128)S(1)}, f32[128,1,1024]{2,0,1:T(8,128)S(1)}, u32[]{:S(2)}, u32[]{:S(2)}) collective-permute-start(f32[128,1,1024]{2,0,1:T(8,128)S(1)} %get-tuple-element.18), channel_id=1, source_target_pairs={{0,1},{1,2},{2,3},{3,4},{4,5},{5,6},{6,7},{7,8},{8,9},{9,10},{10,1... | collective-permute-start | bytes 1572872 | tf_op jit(solution)/shard_map/ppermute | solution.py:101
  5.5 1.3 collective-permute-start.1
  6.8 0.2 convolution_bitcast_fusion
  7.1 4.1 %collective-permute-done.1 = f32[128,1,1024]{2,0,1:T(8,128)S(1)} collective-permute-done((f32[128,1,1024]{2,0,1:T(8,128)S(1)}, f32[128,1,1024]{2,0,1:T(8,128)S(1)}, u32[]{:S(2)}, u32[]{:S(2)}) %collective-permute-start.1) | collective-permute-done | bytes 524320 | tf_op jit(solution)/shard_map/ppermute | solution.py:102
  11.2 2.6 %fusion.8 = f32[128,4,1024]{2,0,1:T(8,128)S(1)} fusion(f32[128,4,1024]{2,0,1:T(8,128)S(1)} %copy.27, f32[128,1,1024]{2,0,1:T(8,128)S(1)} %collective-permute-done.1, f32[128,1,1024]{2,0,1:T(8,128)S(1)} %collective-permute-done, f32[4,1024]{1,0:T(4,128)S(1)} %get-tuple-element.26, f32[4,1024]{1,0:T(4,128)S(1)} %get-tuple-element.27, ...), kind=kLoop, calls=%fused_computation.14 | loop fusion | flops 8388608 | bytes 7405568 | tf_op jit(solution)/shard_map/add | solution.py:116
  13.8 1.3 copy-done.4
  15.1 1.1 fusion.42
  16.1 12.9 %collective-permute-start.2 = (f32[128,1,1024]{2,0,1:T(8,128)}, f32[128,1,1024]{2,0,1:T(8,128)S(1)}, u32[]{:S(2)}, u32[]{:S(2)}) collective-permute-start(f32[128,1,1024]{2,0,1:T(8,128)} %get-tuple-element.16), channel_id=1, source_target_pairs={{0,1},{1,2},{2,3},{3,4},{4,5},{5,6},{6,7},{7,8},{8,9},{9,10},{10,1... | collective-permute-start | bytes 1572872 | tf_op jit(solution)/shard_map/ppermute | solution.py:101
  29.1 1.3 collective-permute-start.3
  30.6 0.2 collective-permute-done.2
  30.8 2.5 %collective-permute-done.3 = f32[128,1,1024]{2,0,1:T(8,128)} collective-permute-done((f32[128,1,1024]{2,0,1:T(8,128)}, f32[128,1,1024]{2,0,1:T(8,128)}, u32[]{:S(2)}, u32[]{:S(2)}) %collective-permute-start.3) | collective-permute-done | bytes 524320 | tf_op jit(solution)/shard_map/ppermute | solution.py:102
  33.2 7.3 %fusion.16 = (f32[128,4,1024]{2,0,1:T(8,128)}, f32[128,4,1024]{2,0,1:T(8,128)}) fusion(f32[128,4,1024]{2,0,1:T(8,128)} %copy-done.4, f32[128,1,1024]{2,0,1:T(8,128)} %collective-permute-done.3, f32[128,1,1024]{2,0,1:T(8,128)S(1)} %collective-permute-done.2, f32[4,1024]{1,0:T(4,128)S(1)} %get-tuple-element.26, f32[4,1024]{1,0:T(4,128)S(1)} %get-tuple-element.27, ...), kind=kLoop, calls=%fused_computation.22 | loop fusion | flops 8388608 | bytes 9502720 | tf_op jit(solution)/shard_map/add | solution.py:116
  40.5 2.9 %copy.28 = f32[128,4,1024]{0,2,1:T(8,128)} copy(f32[128,4,1024]{2,0,1:T(8,128)} %get-tuple-element.14) | data formatting | bytes 4194304 | tf_op jit(solution)/shard_map/add | solution.py:116
  43.4 2.6 %gather_fusion = f32[512,128]{1,0:T(8,128)S(1)} fusion(f32[128,4096]{0,1:T(8,128)} %bitcast.21, s32[1024]{0:T(1024)S(1)} %pad_clamp_fusion), kind=kCustom, calls=%fused_computation | custom fusion | bytes 526336 | tf_op jit(solution)/shard_map/jit(_take)/gather | solution.py:160
  46.1 0.3 subtract_divide_fusion
  46.4 0.6 collective-permute-start.4
  47.0 0.2 select_reduce_fusion
  47.2 5.6 %collective-permute-done.4 = f32[128,512]{0,1:T(8,128)S(1)} collective-permute-done((f32[128,512]{0,1:T(8,128)S(1)}, f32[128,512]{0,1:T(8,128)S(1)}, u32[]{:S(2)}, u32[]{:S(2)}) %collective-permute-start.4) | collective-permute-done | bytes 262176 | tf_op jit(solution)/shard_map/ppermute | solution.py:161
  52.8 2.6 %copy.30 = f32[128,4,1024]{2,0,1:T(8,128)} copy(f32[128,4,1024]{2,1,0:T(4,128)S(1)} %copy-done.1) | data formatting | bytes 4194304 | tf_op jit(solution)/shard_map/optimization_barrier | solution.py:162
  55.4 0.5 collective-permute-start.7
  56.1 0.2 fusion.35
  56.3 1.1 fusion.31
  57.5 12.9 %collective-permute-start.5 = (f32[128,384]{1,0:T(8,128)S(1)}, f32[128,384]{1,0:T(8,128)S(1)}, u32[]{:S(2)}, u32[]{:S(2)}) collective-permute-start(f32[128,384]{1,0:T(8,128)S(1)} %slice_select_fusion), channel_id=1, source_target_pairs={{0,1},{1,0},{2,3},{3,2},{4,5},{5,4},{6,7},{7,6},{8,9},{9,8},{10,11... | collective-permute-start | bytes 589832 | tf_op jit(solution)/shard_map/ppermute | solution.py:126
  70.4 1.1 collective-permute-done.5
  71.6 47.2 %all_to_all.18 = f32[64,2,384]{2,1,0:T(2,128)S(1)} all-to-all(f32[64,2,384]{2,1,0:T(2,128)S(1)} %all_to_all.12), channel_id=1, replica_groups=mesh['member'=2,'z'=8,'y'=4,'xh'=2,'core'=2] {'z','y','xh'}, dimensions={0} | all-to-all | bytes 393216 | tf_op jit(solution)/shard_map/all_to_all | solution.py:128
  119.0 25.6 %all_to_all.19 = f32[64,2,384]{2,1,0:T(2,128)S(1)} all-to-all(f32[64,2,384]{2,1,0:T(2,128)S(1)} %broadcast_in_dim.28), channel_id=1, replica_groups=mesh['member'=2,'z'=8,'y'=4,'xh'=2,'core'=2] {'z','y','xh'}, dimensions={0} | all-to-all | bytes 393216 | tf_op jit(solution)/shard_map/all_to_all | solution.py:131
  144.8 2.7 %copy.35 = f32[128,4,1024]{2,1,0:T(4,128)} copy(f32[128,4,1024]{2,0,1:T(8,128)S(1)} %copy-done.3) | data formatting | bytes 4194304
  147.5 0.8 pad_maximum_fusion.4.g_ref
  148.3 13.7 %solve.1 = f32[256,128]{1,0:T(8,128)} custom-call(f32[256,384]{1,0:T(8,128)} %pad_maximum_fusion.4.g_ref), custom_call_target="tpu_custom_call" | custom-call | flops 200000000 | bytes 600000 | tf_op jit(solution)/shard_map/solve/pallas_call | solution.py:79
  162.0 4.3 %fusion.30 = f32[128,4,1024]{2,0,1:T(8,128)S(1)} fusion(f32[128,4,1024]{2,0,1:T(8,128)S(1)} %copy-done.2, f32[128,4,1024]{2,0,1:T(8,128)} %collective-permute-done.7, f32[256,128]{1,0:T(8,128)} %solve.1), kind=kOutput, calls=%fused_computation.41 | convolution fusion | flops 1613234176 | bytes 6422528 | tf_op jit(solution)/shard_map/kj,kxy->jxy/dot_general | solution.py:176
  166.3 2.7 %copy.34 = f32[128,4,1024]{2,1,0:T(4,128)} copy(f32[128,4,1024]{2,0,1:T(8,128)S(1)} %fusion.30) | data formatting | bytes 4194304
  (40 shorter events, 1.1 us)
Async XLA Ops:
  0.6 6.2 %copy-start = (f32[8,4]{0,1:T(4,128)S(1)}, f32[8,4]{0,1:T(4,128)}, u32[]{:S(2)}) copy-start(f32[8,4]{0,1:T(4,128)} %param.11) | copy-start | bytes 388
  0.6 6.2 %copy-start.6 = (s32[4,1024]{1,0:T(4,128)S(1)}, s32[4,1024]{1,0:T(4,128)}, u32[]{:S(2)}) copy-start(s32[4,1024]{1,0:T(4,128)} %param.10) | copy-start | bytes 49156
  3.5 7.7 %copy-start.1 = (f32[128,4,1024]{2,1,0:T(4,128)S(1)}, f32[128,4,1024]{2,1,0:T(4,128)}, u32[]{:S(2)}) copy-start(f32[128,4,1024]{2,1,0:T(4,128)} %param.8) | copy-start | bytes 6291460
  3.6 3.5 %collective-permute-start = (f32[128,1,1024]{2,0,1:T(8,128)S(1)}, f32[128,1,1024]{2,0,1:T(8,128)S(1)}, u32[]{:S(2)}, u32[]{:S(2)}) collective-permute-start(f32[128,1,1024]{2,0,1:T(8,128)S(1)} %get-tuple-element.18), channel_id=1, source_target_pairs={{0,1},{1,2},{2,3},{3,4},{4,5},{5,6},{6,7},{7,8},{8,9},{9,10},{10,1... | collective-permute-start | bytes 1572872 | tf_op jit(solution)/shard_map/ppermute | solution.py:101
  5.5 5.7 %collective-permute-start.1 = (f32[128,1,1024]{2,0,1:T(8,128)S(1)}, f32[128,1,1024]{2,0,1:T(8,128)S(1)}, u32[]{:S(2)}, u32[]{:S(2)}) collective-permute-start(f32[128,1,1024]{2,0,1:T(8,128)S(1)} %get-tuple-element.19), channel_id=1, source_target_pairs={{1,0},{2,1},{3,2},{4,3},{5,4},{6,5},{7,6},{8,7},{9,8},{10,9},{11,1... | collective-permute-start | bytes 1572872 | tf_op jit(solution)/shard_map/ppermute | solution.py:102
  13.8 1.3 copy-start.4
  15.1 15.3 %copy-start.5 = (f32[128,512]{1,0:T(8,128)S(1)}, f32[128,512]{1,0:T(8,128)}, u32[]{:S(2)}) copy-start(f32[128,512]{1,0:T(8,128)} %param.15) | copy-start | bytes 786436
  15.1 15.4 %copy-start.9 = (s32[512]{0:T(512)S(1)}, s32[512]{0:T(512)}, u32[]{:S(2)}) copy-start(s32[512]{0:T(512)} %param.12) | copy-start | bytes 6148
  16.1 14.6 %collective-permute-start.2 = (f32[128,1,1024]{2,0,1:T(8,128)}, f32[128,1,1024]{2,0,1:T(8,128)S(1)}, u32[]{:S(2)}, u32[]{:S(2)}) collective-permute-start(f32[128,1,1024]{2,0,1:T(8,128)} %get-tuple-element.16), channel_id=1, source_target_pairs={{0,1},{1,2},{2,3},{3,4},{4,5},{5,6},{6,7},{7,8},{8,9},{9,10},{10,1... | collective-permute-start | bytes 1572872 | tf_op jit(solution)/shard_map/ppermute | solution.py:101
  29.1 4.1 %collective-permute-start.3 = (f32[128,1,1024]{2,0,1:T(8,128)}, f32[128,1,1024]{2,0,1:T(8,128)}, u32[]{:S(2)}, u32[]{:S(2)}) collective-permute-start(f32[128,1,1024]{2,0,1:T(8,128)} %get-tuple-element.17), channel_id=1, source_target_pairs={{1,0},{2,1},{3,2},{4,3},{5,4},{6,5},{7,6},{8,7},{9,8},{10,9},{11,1... | collective-permute-start | bytes 1572872 | tf_op jit(solution)/shard_map/ppermute | solution.py:102
  43.4 2.7 %copy-start.7 = (f32[512]{0:T(512)S(1)}, f32[512]{0:T(512)}, u32[]{:S(2)}) copy-start(f32[512]{0:T(512)} %param.14) | copy-start | bytes 6148
  43.4 2.7 %copy-start.8 = (f32[512]{0:T(512)S(1)}, f32[512]{0:T(512)}, u32[]{:S(2)}) copy-start(f32[512]{0:T(512)} %param.13) | copy-start | bytes 6148
  46.4 6.5 %collective-permute-start.4 = (f32[128,512]{0,1:T(8,128)S(1)}, f32[128,512]{0,1:T(8,128)S(1)}, u32[]{:S(2)}, u32[]{:S(2)}) collective-permute-start(f32[128,512]{0,1:T(8,128)S(1)} %get-tuple-element.11), channel_id=1, source_target_pairs={{0,128},{128,0},{1,129},{129,1},{2,130},{130,2},{3,131},{131,3},{4... | collective-permute-start | bytes 786440 | tf_op jit(solution)/shard_map/ppermute | solution.py:161
  55.4 106.6 %collective-permute-start.7 = (f32[128,4,1024]{2,0,1:T(8,128)}, f32[128,4,1024]{2,0,1:T(8,128)}, u32[]{:S(2)}, u32[]{:S(2)}) collective-permute-start(f32[128,4,1024]{2,0,1:T(8,128)} %copy.30), channel_id=1, source_target_pairs={{0,128},{128,0},{1,129},{129,1},{2,130},{130,2},{3,131},{131,3},{4... | collective-permute-start | bytes 6291464 | tf_op jit(solution)/shard_map/ppermute | solution.py:163
  56.3 88.5 %copy-start.3 = (f32[128,4,1024]{2,0,1:T(8,128)S(1)}, f32[128,4,1024]{2,0,1:T(8,128)}, u32[]{:S(2)}) copy-start(f32[128,4,1024]{2,0,1:T(8,128)} %get-tuple-element.14) | copy-start | bytes 6291460
  57.5 14.0 %collective-permute-start.5 = (f32[128,384]{1,0:T(8,128)S(1)}, f32[128,384]{1,0:T(8,128)S(1)}, u32[]{:S(2)}, u32[]{:S(2)}) collective-permute-start(f32[128,384]{1,0:T(8,128)S(1)} %slice_select_fusion), channel_id=1, source_target_pairs={{0,1},{1,0},{2,3},{3,2},{4,5},{5,4},{6,7},{7,6},{8,9},{9,8},{10,11... | collective-permute-start | bytes 589832 | tf_op jit(solution)/shard_map/ppermute | solution.py:126
  144.7 2.8 %collective-permute-start.6 = (f32[128,384]{1,0:T(8,128)S(1)}, f32[128,384]{1,0:T(8,128)S(1)}, u32[]{:S(2)}, u32[]{:S(2)}) collective-permute-start(f32[128,384]{1,0:T(8,128)S(1)} %all_to_all.15), channel_id=1, source_target_pairs={{0,1},{1,0},{2,3},{3,2},{4,5},{5,4},{6,7},{7,6},{8,9},{9,8},{10,11... | collective-permute-start | bytes 589832 | tf_op jit(solution)/shard_map/ppermute | solution.py:132
  147.4 14.5 %copy-start.2 = (f32[128,4,1024]{2,0,1:T(8,128)S(1)}, f32[128,4,1024]{2,0,1:T(8,128)}, u32[]{:S(2)}) copy-start(f32[128,4,1024]{2,0,1:T(8,128)} %get-tuple-element.15) | copy-start | bytes 6291460

commit v3 on v2

--- a/solution.py
+++ b/solution.py
@@ -93,27 +93,36 @@
     return jnp.einsum("rd,rxy->dxy", regime_coefs, onehot, precision=lax.Precision.HIGHEST)
 
 
-def with_halo(cells):
-    count = lax.axis_size(SPACE)
-    ends = count - 1
-    head = cells[:, :1]
-    tail = cells[:, -1:]
+def halo(head, tail):
+    ends = lax.axis_size(SPACE) - 1
     above = lax.ppermute(tail, SPACE, [(i, i + 1) for i in range(ends)])
     below = lax.ppermute(head, SPACE, [(i + 1, i) for i in range(ends)])
-    return jnp.concatenate([above, cells, below], axis=1)
-
-
-def advance(extended, rates, coefs):
-    center = extended[..., 1:-1, :]
-    widths = [(0, 0)] * (center.ndim - 1) + [(1, 1)]
-    padded_cols = jnp.pad(center, widths)
-    above = extended[..., :-2, :]
-    below = extended[..., 2:, :]
-    left_side = padded_cols[..., :-2]
-    right_side = padded_cols[..., 2:]
-    flow = coefs[0] * (above - center) + coefs[1] * (below - center)
-    flow = flow + coefs[2] * (left_side - center) + coefs[3] * (right_side - center)
-    return center + rates * flow
+    return above, below
+
+
+def advance(above, center, below, rate, coef):
+    padded = jnp.pad(center, ((0, 0), (1, 1)))
+    flow = coef[0] * (above - center) + coef[1] * (below - center)
+    flow = flow + coef[2] * (padded[:, :-2] - center) + coef[3] * (padded[:, 2:] - center)
+    return center + rate * flow
+
+
+def two_steps(rows, rates, coefs):
+    last = len(rows) - 1
+    above, below = halo(rows[0], rows[last])
+    for repeat in range(2):
+        ends = (
+            advance(above, rows[0], rows[1], rates[0], coefs[0]),
+            advance(rows[last - 1], rows[last], below, rates[last], coefs[last]),
+        )
+        inner = [
+            advance(rows[r - 1], rows[r], rows[r + 1], rates[r], coefs[r]) for r in range(1, last)
+        ]
+        if repeat == 0:
+            ends = lax.optimization_barrier(ends)
+            above, below = halo(*ends)
+        rows = [ends[0], *inner, ends[1]]
+    return rows, below
 
 
 def reduce_over_space(block):
@@ -130,9 +139,10 @@
     spread = jnp.broadcast_to(piece[None], (chips,) + piece.shape).reshape(half, -1)
     summed = lax.all_to_all(spread, CHIPS, 0, 0, tiled=True)
     other = lax.ppermute(summed, "core", SWAP)
-    return jnp.concatenate(
+    whole = jnp.concatenate(
         [jnp.where(first, summed, other), jnp.where(first, other, summed)], axis=0
     )
+    return whole, summed
 
 
 def strip(
@@ -150,31 +160,51 @@
     columns = params.shape[2]
     members = own * lax.axis_size("member")
     square_root_scale = math.sqrt(members - 1)
-    coefs = coef_fields(regime, regime_coefs)
-    rates = time_step * jnp.exp(params)
-    current = state
-    for _ in range(2):
-        current = advance(with_halo(current), rates, coefs)
+    fields = coef_fields(regime, regime_coefs)
+    coefs = [fields[:, r] for r in range(strip_rows)]
+    by_row = lax.optimization_barrier(jnp.swapaxes(params, 0, 1))
+    state_rows = lax.optimization_barrier(jnp.swapaxes(state, 0, 1))
+    own_rows = [by_row[r] for r in range(strip_rows)]
+    rates = [time_step * jnp.exp(row) for row in own_rows]
+    rows, edge = two_steps([state_rows[r] for r in range(strip_rows)], rates, coefs)
+
+    def swap(row, after):
+        row, after = lax.optimization_barrier((own_rows[row], after))
+        return lax.ppermute(row, "member", SWAP), after
+
     local_index = observation_index - lax.axis_index(SPACE) * (strip_rows * columns)
-    flat = current.reshape(own, strip_rows * columns)
-    mine = jnp.take(flat, local_index, axis=1)
+    mine = jnp.take(jnp.concatenate(rows, axis=1), local_index, axis=1, mode="clip")
+    swapped = [swap(0, edge)[0]]
     theirs = lax.ppermute(mine, "member", SWAP)
-    params_there, theirs2 = lax.optimization_barrier((params, theirs))
-    other_params = lax.ppermute(params_there, "member", SWAP)
-    predicted = jnp.concatenate([mine, theirs2], axis=0)
-    mean = jnp.sum(predicted, axis=0) / members
+    other, theirs = swap(1, theirs)
+    swapped.append(other)
+    mean = (jnp.sum(mine, axis=0) + jnp.sum(theirs, axis=0)) / members
+    predicted = jnp.concatenate([mine, theirs], axis=0)
     anomalies = (predicted - mean[None, :]) / (observation_spread[None, :] * square_root_scale)
     innovations = (
         measured_values[None, :] + observation_spread[None, :] * observation_jitter - mine
     ) / observation_spread[None, :]
     stacked = jnp.concatenate([anomalies, innovations], axis=0)
-    rows = jnp.dot(
+    products = jnp.dot(
         anomalies, stacked.T, precision=HIGHEST, preferred_element_type=jnp.float32
     )
-    mixing = solve(reduce_over_space(rows))
-    both = jnp.concatenate([params, other_params], axis=0) / square_root_scale
-    update = jnp.einsum("kj,kxy->jxy", mixing, both, precision=lax.Precision.HIGHEST)
-    return (params + update, current)
+    whole, summed = reduce_over_space(products)
+    for r in range(2, strip_rows):
+        other, summed = swap(r, summed)
+        swapped.append(other)
+    mixing = solve(whole) / square_root_scale
+    revised = [
+        own_rows[r]
+        + lax.dot_general(
+            mixing,
+            jnp.concatenate([own_rows[r], swapped[r]], axis=0),
+            (((0,), (0,)), ((), ())),
+            precision=HIGHEST,
+            preferred_element_type=jnp.float32,
+        )
+        for r in range(strip_rows)
+    ]
+    return (jnp.stack(revised, axis=1), jnp.stack(rows, axis=1))
 
 
 def solution(mesh):

time: 172 us -> 162 us (0.942)
  blocking collectives: 72.8 us -> 49.2 us
  waiting for transfers between devices: 13.4 us -> 26.2 us
  matrix products: 5.6 us -> 7.92 us
  starting transfers between devices: 31.6 us -> 29.7 us
    all_to_all x1, blocking collectives: 47.2 us -> 31.4 us  [reduce_over_space(): pieces = lax.all_to_all(part, CHIPS, 0, 0, tiled=True)]
    ppermute x5 -> x8, waiting for transfers between devices: 6.7 us -> 21.9 us  [the longest x4 19 us: swap(): return (lax.ppermute(row, 'member', SWAP), after)]
    all_to_all x1, blocking collectives: 25.6 us -> 17.8 us  [reduce_over_space(): summed = lax.all_to_all(spread, CHIPS, 0, 0, tiled=True)]
    ppermute x1, starting transfers between devices: 12.9 us -> 6.65 us  [reduce_over_space(): part = kept + lax.ppermute(sent, 'core', SWAP)]
    add x2 -> x4, other arithmetic: 9.88 us -> 5.42 us  [advance(): return center + rate * flow]
    ppermute x5 -> x8, starting transfers between devices: 17.9 us -> 22.3 us  [the longest x2 15.6 us: halo(): above = lax.ppermute(tail, SPACE, [(i, i + 1) for i in range(ends)])]
    add x1 -> x0, local copies, waits for them, and re-layouts: 2.88 us -> none  [advance(): return center + rates * flow]
    concatenate x0 -> x1, local copies, waits for them, and re-layouts: none -> 2.88 us  [strip(): jnp.concatenate(rows, axis=1)]
  transfers between devices with their start and end apart: 8 -> 11, of which waited for: 5 -> 6; matrix products, arithmetic and copies ran while one was open for 3% -> 12% of each run, Pallas kernels for 8% -> 9%
where the time goes in v3:
time: 162 us; the launch traced here: 160 us
  blocking collectives  49.2 us (30%)
  starting transfers between devices  29.7 us (18%)
  waiting for transfers between devices  26.2 us (16%)
  local copies, waits for them, and re-layouts  19.9 us (12%)
  Pallas kernels  13.7 us (8%)
  other arithmetic  12.4 us (8%)
  matrix products  7.92 us (5%)
    all_to_all x1, blocking collectives, reduce_over_space(): pieces = lax.all_to_all(part, CHIPS, 0, 0, tiled=True)  31.4 us
    ppermute x4, waiting for transfers between devices, swap(): return (lax.ppermute(row, 'member', SWAP), after)  19 us
    all_to_all x1, blocking collectives, reduce_over_space(): summed = lax.all_to_all(spread, CHIPS, 0, 0, tiled=True)  17.8 us
    ppermute x2, starting transfers between devices, halo(): above = lax.ppermute(tail, SPACE, [(i, i + 1) for i in range(ends)])  15.6 us
    pallas_call x1, Pallas kernels, solve(): pl.pallas_call(solve_kernel, out_shape=jax.ShapeDtypeStruct((m, wide - m)...  13.7 us
    unnamed x37, local copies, waits for them, and re-layouts  11.6 us
    ppermute x1, starting transfers between devices, reduce_over_space(): part = kept + lax.ppermute(sent, 'core', SWAP)  6.65 us
    dot_general x4, matrix products, strip(): lax.dot_general(mixing, jnp.concatenate([own_rows[r], swapped[r]], axis=0...  6.64 us
  transfers between devices with their start and end apart: 11, of which 6 were waited for; matrix products, arithmetic and copies ran while one was open for 12% of the time, Pallas kernels for 9%

profile of v3, /device:TPU:2, one launch (start us, length us, event | category | flops | bytes accessed | tf_op | source)
XLA Modules:
  0.0 160.1 jit_solution(17444594405677625397)
XLA Ops:
  0.6 2.8 %copy.18 = f32[128,4,1024]{2,0,1:T(8,128)S(1)} copy(f32[128,4,1024]{2,1,0:T(4,128)} %param.9) | data formatting | bytes 4194304 | tf_op args[1]
  3.5 1.2 slice_bitcast_fusion.2
  4.7 1.9 %collective-permute-start = (f32[128,1024]{1,0:T(8,128)S(1)}, f32[128,1024]{1,0:T(8,128)S(1)}, u32[]{:S(2)}, u32[]{:S(2)}) collective-permute-start(f32[128,1024]{1,0:T(8,128)S(1)} %get-tuple-element.30), channel_id=1, source_target_pairs={{0,1},{1,2},{2,3},{3,4},{4,5},{5,6},{6,7},{7,8},{8,9},{9,10},{10,1... | collective-permute-start | bytes 1572872 | tf_op jit(solution)/shard_map/ppermute | solution.py:98
  6.6 1.3 collective-permute-start.1
  7.9 1.2 copy.19
  9.5 2.9 %collective-permute-done.1 = f32[128,1024]{1,0:T(8,128)S(1)} collective-permute-done((f32[128,1024]{1,0:T(8,128)S(1)}, f32[128,1024]{1,0:T(8,128)S(1)}, u32[]{:S(2)}, u32[]{:S(2)}) %collective-permute-start.1) | collective-permute-done | bytes 524320 | tf_op jit(solution)/shard_map/ppermute | solution.py:99
  13.2 13.7 %collective-permute-start.2 = (f32[128,1024]{1,0:T(8,128)S(1)}, f32[128,1024]{1,0:T(8,128)}, u32[]{:S(2)}, u32[]{:S(2)}) collective-permute-start(f32[128,1024]{1,0:T(8,128)S(1)} %get-tuple-element.9), channel_id=1, source_target_pairs={{0,1},{1,2},{2,3},{3,4},{4,5},{5,6},{6,7},{7,8},{8,9},{9,10},{10,1... | collective-permute-start | bytes 1572872 | tf_op jit(solution)/shard_map/ppermute | solution.py:98
  26.9 1.3 collective-permute-start.3
  28.2 2.9 %fusion.49 = (f32[128,1024]{1,0:T(8,128)S(1)}, f32[128,1024]{1,0:T(8,128)S(1)}) fusion(f32[128,1024]{1,0:T(8,128)S(1)} %get-tuple-element.8, f32[128,1024]{1,0:T(8,128)} %collective-permute-done.2, f32[1024]{0:T(1024)S(1)} %bitcast.116, f32[1024]{0:T(1024)S(1)} %bitcast.118, f32[1024]{0:T(1024)S(1)} %bitcast.120, f32[1024]{0:T(1024)S(1)} %bitcast.122, ...), kind=kLoop, calls=%fused_computation.76 | loop fusion | flops 3670016 | bytes 4751360 | tf_op jit(solution)/shard_map/add | solution.py:107
  34.0 1.5 pad_maximum_fusion
  35.5 2.9 %copy.12 = f32[128,4096]{0,1:T(8,128)} copy(f32[128,4096]{1,0:T(8,128)} %pad_maximum_fusion) | data formatting | bytes 4194304 | tf_op jit(solution)/shard_map/concatenate | solution.py:176
  38.4 2.6 %gather_fusion = f32[512,128]{1,0:T(8,128)S(1)} fusion(f32[128,4096]{0,1:T(8,128)} %copy.12, s32[1024]{0:T(1024)S(1)} %pad_clamp_fusion), kind=kCustom, calls=%fused_computation | custom fusion | bytes 526336 | tf_op jit(solution)/shard_map/jit(_take)/gather | solution.py:176
  41.7 1.2 slice_bitcast_fusion.7
  44.4 3.2 %collective-permute-done.4 = f32[128,512]{0,1:T(8,128)} collective-permute-done((f32[128,512]{0,1:T(8,128)S(1)}, f32[128,512]{0,1:T(8,128)}, u32[]{:S(2)}, u32[]{:S(2)}) %collective-permute-start.4) | collective-permute-done | bytes 262176 | tf_op jit(solution)/shard_map/ppermute | solution.py:178
  47.6 1.1 reduce_sum.28
  48.7 1.2 fusion.84
  49.9 1.1 fusion.16
  51.0 6.7 %collective-permute-start.5 = (f32[128,384]{1,0:T(8,128)S(1)}, f32[128,384]{1,0:T(8,128)S(1)}, u32[]{:S(2)}, u32[]{:S(2)}) collective-permute-start(f32[128,384]{1,0:T(8,128)S(1)} %slice_select_fusion), channel_id=1, source_target_pairs={{0,1},{1,0},{2,3},{3,2},{4,5},{5,4},{6,7},{7,6},{8,9},{9,8},{10,11... | collective-permute-start | bytes 589832 | tf_op jit(solution)/shard_map/ppermute | solution.py:135
  58.9 31.4 %all_to_all.18 = f32[64,2,384]{2,1,0:T(2,128)S(1)} all-to-all(f32[64,2,384]{2,1,0:T(2,128)S(1)} %all_to_all.12), channel_id=1, replica_groups=mesh['member'=2,'z'=8,'y'=4,'xh'=2,'core'=2] {'z','y','xh'}, dimensions={0} | all-to-all | bytes 393216 | tf_op jit(solution)/shard_map/all_to_all | solution.py:137
  90.5 17.8 %all_to_all.19 = f32[64,2,384]{2,1,0:T(2,128)S(1)} all-to-all(f32[64,2,384]{2,1,0:T(2,128)S(1)} %broadcast_in_dim.7), channel_id=1, replica_groups=mesh['member'=2,'z'=8,'y'=4,'xh'=2,'core'=2] {'z','y','xh'}, dimensions={0} | all-to-all | bytes 393216 | tf_op jit(solution)/shard_map/all_to_all | solution.py:140
  109.5 1.1 collective-permute-start.7
  110.6 1.8 %pad_maximum_fusion.2 = f32[128,4,1024]{2,0,1:T(8,128)S(1)} fusion(f32[128,1,1024]{2,0,1:T(8,128)} %bitcast.104, f32[128,1,1024]{2,0,1:T(8,128)} %bitcast.103, f32[128,1,1024]{2,0,1:T(8,128)} %bitcast.102, f32[128,1,1024]{2,0,1:T(8,128)} %bitcast.101), kind=kLoop, calls=%fused_computation.3 | loop fusion | flops 1572864 | bytes 4194304 | tf_op jit(solution)/shard_map/stack | solution.py:207
  112.4 2.7 %copy.15 = f32[128,4,1024]{2,1,0:T(4,128)} copy(f32[128,4,1024]{2,0,1:T(8,128)S(1)} %pad_maximum_fusion.2) | data formatting | bytes 4194304
  116.0 1.1 collective-permute-start.9
  117.9 13.7 %solve.1 = f32[256,128]{1,0:T(8,128)} custom-call(f32[256,384]{1,0:T(8,128)} %pad_maximum_fusion.3.g_ref), custom_call_target="tpu_custom_call" | custom-call | flops 200000000 | bytes 600000 | tf_op jit(solution)/shard_map/solve/pallas_call | solution.py:79
  131.6 3.1 %collective-permute-done.7 = f32[128,1024]{1,0:T(8,128)} collective-permute-done((f32[128,1024]{1,0:T(8,128)}, f32[128,1024]{1,0:T(8,128)}, u32[]{:S(2)}, u32[]{:S(2)}) %collective-permute-start.7) | collective-permute-done | bytes 524320 | tf_op jit(solution)/shard_map/ppermute | solution.py:173
  134.7 2.2 %fusion = f32[128,1,1024]{2,0,1:T(8,128)S(1)} fusion(f32[128,1024]{1,0:T(8,128)} %get-tuple-element.11, f32[128,1024]{1,0:T(8,128)} %collective-permute-done.7, f32[256,128]{1,0:T(8,128)} %solve.1), kind=kOutput, calls=%fused_computation.10 | convolution fusion | flops 403079168 | bytes 1703936 | tf_op jit(solution)/shard_map/dot_general | solution.py:198
  136.9 9.0 %collective-permute-done.8 = f32[128,1024]{1,0:T(8,128)S(1)} collective-permute-done((f32[128,1024]{1,0:T(8,128)}, f32[128,1024]{1,0:T(8,128)S(1)}, u32[]{:S(2)}, u32[]{:S(2)}) %collective-permute-start.8) | collective-permute-done | bytes 524320 | tf_op jit(solution)/shard_map/ppermute | solution.py:173
  145.9 2.0 %fusion.1 = f32[128,1,1024]{2,0,1:T(8,128)S(1)} fusion(f32[128,1024]{1,0:T(8,128)} %get-tuple-element.12, f32[128,1024]{1,0:T(8,128)S(1)} %collective-permute-done.8, f32[256,128]{1,0:T(8,128)S(1)} %copy-done.7), kind=kOutput, calls=%fused_computation.11 | convolution fusion | flops 403079168 | bytes 1703936 | tf_op jit(solution)/shard_map/dot_general | solution.py:198
  147.8 1.8 %fusion.3 = f32[128,1,1024]{2,0,1:T(8,128)S(1)} fusion(f32[128,1024]{1,0:T(8,128)S(1)} %get-tuple-element.27, f32[128,1024]{1,0:T(8,128)} %collective-permute-done.10, f32[256,128]{1,0:T(8,128)S(1)} %copy-done.7), kind=kOutput, calls=%fused_computation.13 | convolution fusion | flops 403079168 | bytes 1703936 | tf_op jit(solution)/shard_map/dot_general | solution.py:198
  149.6 6.9 %collective-permute-done.9 = f32[128,1024]{1,0:T(8,128)S(1)} collective-permute-done((f32[128,1024]{1,0:T(8,128)S(1)}, f32[128,1024]{1,0:T(8,128)S(1)}, u32[]{:S(2)}, u32[]{:S(2)}) %collective-permute-start.9) | collective-permute-done | bytes 524320 | tf_op jit(solution)/shard_map/ppermute | solution.py:173
  157.4 2.7 %copy.14 = f32[128,4,1024]{2,1,0:T(4,128)} copy(f32[128,4,1024]{2,0,1:T(8,128)S(1)} %pad_maximum_fusion.1) | data formatting | bytes 4194304
  (63 shorter events, 11.3 us)
Async XLA Ops:
  0.6 8.5 %copy-start = (f32[8,4]{0,1:T(4,128)S(1)}, f32[8,4]{0,1:T(4,128)}, u32[]{:S(2)}) copy-start(f32[8,4]{0,1:T(4,128)} %param.11) | copy-start | bytes 388
  3.5 8.9 %copy-start.1 = (f32[128,4,1024]{2,0,1:T(8,128)}, f32[128,4,1024]{2,0,1:T(8,128)S(1)}, u32[]{:S(2)}) copy-start(f32[128,4,1024]{2,0,1:T(8,128)S(1)} %copy.18) | copy-start | bytes 6291460
  3.5 4.5 %copy-start.8 = (f32[128,4,1024]{2,1,0:T(4,128)S(1)}, f32[128,4,1024]{2,1,0:T(4,128)}, u32[]{:S(2)}) copy-start(f32[128,4,1024]{2,1,0:T(4,128)} %param.8) | copy-start | bytes 6291460
  4.7 4.7 %collective-permute-start = (f32[128,1024]{1,0:T(8,128)S(1)}, f32[128,1024]{1,0:T(8,128)S(1)}, u32[]{:S(2)}, u32[]{:S(2)}) collective-permute-start(f32[128,1024]{1,0:T(8,128)S(1)} %get-tuple-element.30), channel_id=1, source_target_pairs={{0,1},{1,2},{2,3},{3,4},{4,5},{5,6},{6,7},{7,8},{8,9},{9,10},{10,1... | collective-permute-start | bytes 1572872 | tf_op jit(solution)/shard_map/ppermute | solution.py:98
  6.6 2.6 %copy-start.12 = (s32[4,1024]{1,0:T(4,128)S(1)}, s32[4,1024]{1,0:T(4,128)}, u32[]{:S(2)}) copy-start(s32[4,1024]{1,0:T(4,128)} %param.10) | copy-start | bytes 49156
  6.6 5.7 %collective-permute-start.1 = (f32[128,1024]{1,0:T(8,128)S(1)}, f32[128,1024]{1,0:T(8,128)S(1)}, u32[]{:S(2)}, u32[]{:S(2)}) collective-permute-start(f32[128,1024]{1,0:T(8,128)S(1)} %get-tuple-element.31), channel_id=1, source_target_pairs={{1,0},{2,1},{3,2},{4,3},{5,4},{6,5},{7,6},{8,7},{9,8},{10,9},{11,1... | collective-permute-start | bytes 1572872 | tf_op jit(solution)/shard_map/ppermute | solution.py:99
  12.3 14.6 %copy-start.15 = (s32[512]{0:T(512)S(1)}, s32[512]{0:T(512)}, u32[]{:S(2)}) copy-start(s32[512]{0:T(512)} %param.12) | copy-start | bytes 6148
  13.2 15.0 %copy-start.10 = (f32[128,1024]{1,0:T(8,128)}, f32[128,1024]{1,0:T(8,128)S(1)}, u32[]{:S(2)}) copy-start(f32[128,1024]{1,0:T(8,128)S(1)} %get-tuple-element.9) | copy-start | bytes 1572868
  13.2 15.0 %collective-permute-start.2 = (f32[128,1024]{1,0:T(8,128)S(1)}, f32[128,1024]{1,0:T(8,128)}, u32[]{:S(2)}, u32[]{:S(2)}) collective-permute-start(f32[128,1024]{1,0:T(8,128)S(1)} %get-tuple-element.9), channel_id=1, source_target_pairs={{0,1},{1,2},{2,3},{3,4},{4,5},{5,6},{6,7},{7,8},{8,9},{9,10},{10,1... | collective-permute-start | bytes 1572872 | tf_op jit(solution)/shard_map/ppermute | solution.py:98
  26.9 5.2 %collective-permute-start.3 = (f32[128,1024]{1,0:T(8,128)S(1)}, f32[128,1024]{1,0:T(8,128)S(1)}, u32[]{:S(2)}, u32[]{:S(2)}) collective-permute-start(f32[128,1024]{1,0:T(8,128)S(1)} %get-tuple-element.8), channel_id=1, source_target_pairs={{1,0},{2,1},{3,2},{4,3},{5,4},{6,5},{7,6},{8,7},{9,8},{10,9},{11,1... | collective-permute-start | bytes 1572872 | tf_op jit(solution)/shard_map/ppermute | solution.py:99
  28.2 2.9 %copy-start.2 = (f32[128,4,1024]{2,0,1:T(8,128)S(1)}, f32[128,4,1024]{2,0,1:T(8,128)}, u32[]{:S(2)}) copy-start(f32[128,4,1024]{2,0,1:T(8,128)} %copy-done.1) | copy-start | bytes 6291460
  28.2 2.9 %copy-start.9 = (f32[128,1024]{1,0:T(8,128)S(1)}, f32[128,1024]{1,0:T(8,128)}, u32[]{:S(2)}) copy-start(f32[128,1024]{1,0:T(8,128)} %get-tuple-element.28) | copy-start | bytes 1572868
  31.1 2.1 %copy-start.3 = (f32[128,1024]{1,0:T(8,128)}, f32[128,1024]{1,0:T(8,128)S(1)}, u32[]{:S(2)}) copy-start(f32[128,1024]{1,0:T(8,128)S(1)} %get-tuple-element.16) | copy-start | bytes 1572868
  31.2 1.2 copy-start.11
  32.1 1.2 copy-start.4
  33.2 0.8 copy-start.6
  33.2 2.3 %copy-start.5 = (f32[128,1024]{1,0:T(8,128)}, f32[128,1024]{1,0:T(8,128)S(1)}, u32[]{:S(2)}) copy-start(f32[128,1024]{1,0:T(8,128)S(1)} %get-tuple-element.22) | copy-start | bytes 1572868
  41.0 3.1 %copy-start.13 = (f32[512]{0:T(512)S(1)}, f32[512]{0:T(512)}, u32[]{:S(2)}) copy-start(f32[512]{0:T(512)} %param.14) | copy-start | bytes 6148
  41.0 3.1 %copy-start.14 = (f32[512]{0:T(512)S(1)}, f32[512]{0:T(512)}, u32[]{:S(2)}) copy-start(f32[512]{0:T(512)} %param.13) | copy-start | bytes 6148
  41.0 6.6 %collective-permute-start.4 = (f32[128,512]{0,1:T(8,128)S(1)}, f32[128,512]{0,1:T(8,128)}, u32[]{:S(2)}, u32[]{:S(2)}) collective-permute-start(f32[128,512]{0,1:T(8,128)S(1)} %bitcast.105), channel_id=1, source_target_pairs={{0,128},{128,0},{1,129},{129,1},{2,130},{130,2},{3,131},{131,3},{4... | collective-permute-start | bytes 786440 | tf_op jit(solution)/shard_map/ppermute | solution.py:178
  51.0 7.7 %collective-permute-start.5 = (f32[128,384]{1,0:T(8,128)S(1)}, f32[128,384]{1,0:T(8,128)S(1)}, u32[]{:S(2)}, u32[]{:S(2)}) collective-permute-start(f32[128,384]{1,0:T(8,128)S(1)} %slice_select_fusion), channel_id=1, source_target_pairs={{0,1},{1,0},{2,3},{3,2},{4,5},{5,4},{6,7},{7,6},{8,9},{9,8},{10,11... | collective-permute-start | bytes 589832 | tf_op jit(solution)/shard_map/ppermute | solution.py:135
  108.4 8.7 %collective-permute-start.6 = (f32[128,384]{1,0:T(8,128)S(1)}, f32[128,384]{1,0:T(8,128)S(1)}, u32[]{:S(2)}, u32[]{:S(2)}) collective-permute-start(f32[128,384]{1,0:T(8,128)S(1)} %all_to_all.15), channel_id=1, source_target_pairs={{0,1},{1,0},{2,3},{3,2},{4,5},{5,4},{6,7},{7,6},{8,9},{9,8},{10,11... | collective-permute-start | bytes 589832 | tf_op jit(solution)/shard_map/ppermute | solution.py:141
  108.5 39.3 %collective-permute-start.10 = (f32[128,1024]{1,0:T(8,128)S(1)}, f32[128,1024]{1,0:T(8,128)}, u32[]{:S(2)}, u32[]{:S(2)}) collective-permute-start(f32[128,1024]{1,0:T(8,128)S(1)} %get-tuple-element.27), channel_id=1, source_target_pairs={{0,128},{128,0},{1,129},{129,1},{2,130},{130,2},{3,131},{131,3},{4... | collective-permute-start | bytes 1572872 | tf_op jit(solution)/shard_map/ppermute | solution.py:173
  109.5 25.2 %collective-permute-start.7 = (f32[128,1024]{1,0:T(8,128)}, f32[128,1024]{1,0:T(8,128)}, u32[]{:S(2)}, u32[]{:S(2)}) collective-permute-start(f32[128,1024]{1,0:T(8,128)} %get-tuple-element.11), channel_id=1, source_target_pairs={{0,128},{128,0},{1,129},{129,1},{2,130},{130,2},{3,131},{131,3},{4... | collective-permute-start | bytes 1572872 | tf_op jit(solution)/shard_map/ppermute | solution.py:173
  115.0 30.8 %collective-permute-start.8 = (f32[128,1024]{1,0:T(8,128)}, f32[128,1024]{1,0:T(8,128)S(1)}, u32[]{:S(2)}, u32[]{:S(2)}) collective-permute-start(f32[128,1024]{1,0:T(8,128)} %get-tuple-element.12), channel_id=1, source_target_pairs={{0,128},{128,0},{1,129},{129,1},{2,130},{130,2},{3,131},{131,3},{4... | collective-permute-start | bytes 1572872 | tf_op jit(solution)/shard_map/ppermute | solution.py:173
  116.0 40.5 %collective-permute-start.9 = (f32[128,1024]{1,0:T(8,128)S(1)}, f32[128,1024]{1,0:T(8,128)S(1)}, u32[]{:S(2)}, u32[]{:S(2)}) collective-permute-start(f32[128,1024]{1,0:T(8,128)S(1)} %get-tuple-element.13), channel_id=1, source_target_pairs={{0,128},{128,0},{1,129},{129,1},{2,130},{130,2},{3,131},{131,3},{4... | collective-permute-start | bytes 1572872 | tf_op jit(solution)/shard_map/ppermute | solution.py:173
  131.6 14.3 %copy-start.7 = (f32[256,128]{1,0:T(8,128)S(1)}, f32[256,128]{1,0:T(8,128)}, u32[]{:S(2)}) copy-start(f32[256,128]{1,0:T(8,128)} %solve.1) | copy-start | bytes 393220

commit v4 on v3

--- a/solution.py
+++ b/solution.py
@@ -13,6 +13,7 @@
 SWAP = [(0, 1), (1, 0)]
 HIGHEST = lax.Precision.HIGHEST
 BLOCK = 64
+PARTS = 2
 
 
 def invert_block(block):
@@ -87,6 +88,85 @@
     )(system)
 
 
+def split_kernel(x_ref, *out_refs):
+    for r, out_ref in enumerate(out_refs):
+        out_ref[...] = x_ref[:, r, :]
+
+
+def split_rows(x):
+    m, rows, cols = x.shape
+    return pl.pallas_call(
+        split_kernel,
+        grid=(PARTS,),
+        out_shape=[jax.ShapeDtypeStruct((m, cols), jnp.float32)] * rows,
+        in_specs=[pl.BlockSpec((m // PARTS, rows, cols), lambda i: (i, 0, 0))],
+        out_specs=[pl.BlockSpec((m // PARTS, cols), lambda i: (i, 0))] * rows,
+        cost_estimate=pl.CostEstimate(flops=0, bytes_accessed=8 * x.size, transcendentals=0),
+        name="split_rows",
+    )(x)
+
+
+def merge_kernel(*refs):
+    for r, x_ref in enumerate(refs[:-1]):
+        refs[-1][:, r, :] = x_ref[...]
+
+
+def merge_rows(rows):
+    m, cols = rows[0].shape
+    count = len(rows)
+    return pl.pallas_call(
+        merge_kernel,
+        grid=(PARTS,),
+        out_shape=jax.ShapeDtypeStruct((m, count, cols), jnp.float32),
+        in_specs=[pl.BlockSpec((m // PARTS, cols), lambda i: (i, 0))] * count,
+        out_specs=pl.BlockSpec((m // PARTS, count, cols), lambda i: (i, 0, 0)),
+        cost_estimate=pl.CostEstimate(
+            flops=0, bytes_accessed=8 * count * m * cols, transcendentals=0
+        ),
+        name="merge_rows",
+    )(*rows)
+
+
+def finish_kernel(mix_ref, own_ref, first_ref, second_ref, rest_ref, out_ref):
+    m, rows, _ = own_ref.shape
+    dims = (((0,), (0,)), ((), ()))
+    mix = mix_ref[...] * (1.0 / math.sqrt(2 * m - 1))
+    low, high = mix[:m, :], mix[m:, :]
+    for r in range(rows):
+        mine = own_ref[:, r, :]
+        other = (first_ref, second_ref)[r][...] if r < 2 else rest_ref[r - 2]
+        out_ref[:, r, :] = mine + (
+            lax.dot_general(low, mine, dims, precision=HIGHEST, preferred_element_type=jnp.float32)
+            + lax.dot_general(
+                high, other, dims, precision=HIGHEST, preferred_element_type=jnp.float32
+            )
+        )
+
+
+def finish(mixing, params, first, second, rest):
+    m, rows, cols = params.shape
+    piece = cols // PARTS
+    flat = pl.BlockSpec((m, piece), lambda i: (0, i))
+    whole = pl.BlockSpec((m, rows, piece), lambda i: (0, 0, i))
+    return pl.pallas_call(
+        finish_kernel,
+        grid=(PARTS,),
+        out_shape=jax.ShapeDtypeStruct((m, rows, cols), jnp.float32),
+        in_specs=[
+            pl.BlockSpec((2 * m, m), lambda i: (0, 0)),
+            whole,
+            flat,
+            flat,
+            pl.BlockSpec((rows - 2, m, piece), lambda i: (0, 0, i)),
+        ],
+        out_specs=whole,
+        cost_estimate=pl.CostEstimate(
+            flops=4 * m * m * rows * cols, bytes_accessed=12 * params.size, transcendentals=0
+        ),
+        name="finish",
+    )(mixing, params, first, second, rest)
+
+
 def coef_fields(regime, regime_coefs):
     levels = jnp.arange(regime_coefs.shape[0], dtype=jnp.int32)
     onehot = (regime[None, :, :] == levels[:, None, None]).astype(jnp.float32)
@@ -122,7 +202,7 @@
             ends = lax.optimization_barrier(ends)
             above, below = halo(*ends)
         rows = [ends[0], *inner, ends[1]]
-    return rows, below
+    return rows, (above, below)
 
 
 def reduce_over_space(block):
@@ -142,7 +222,7 @@
     whole = jnp.concatenate(
         [jnp.where(first, summed, other), jnp.where(first, other, summed)], axis=0
     )
-    return whole, summed
+    return whole, other
 
 
 def strip(
@@ -163,21 +243,20 @@
     fields = coef_fields(regime, regime_coefs)
     coefs = [fields[:, r] for r in range(strip_rows)]
     by_row = lax.optimization_barrier(jnp.swapaxes(params, 0, 1))
-    state_rows = lax.optimization_barrier(jnp.swapaxes(state, 0, 1))
     own_rows = [by_row[r] for r in range(strip_rows)]
     rates = [time_step * jnp.exp(row) for row in own_rows]
-    rows, edge = two_steps([state_rows[r] for r in range(strip_rows)], rates, coefs)
-
-    def swap(row, after):
-        row, after = lax.optimization_barrier((own_rows[row], after))
-        return lax.ppermute(row, "member", SWAP), after
+    rows, edge = two_steps(split_rows(state), rates, coefs)
+
+    def swap(piece, after):
+        piece, after = lax.optimization_barrier((piece, after))
+        return lax.ppermute(piece, "member", SWAP), after
 
     local_index = observation_index - lax.axis_index(SPACE) * (strip_rows * columns)
     mine = jnp.take(jnp.concatenate(rows, axis=1), local_index, axis=1, mode="clip")
-    swapped = [swap(0, edge)[0]]
+    first, _ = swap(own_rows[0], edge)
+    predicted_state = merge_rows(rows)
     theirs = lax.ppermute(mine, "member", SWAP)
-    other, theirs = swap(1, theirs)
-    swapped.append(other)
+    second, theirs = swap(own_rows[1], theirs)
     mean = (jnp.sum(mine, axis=0) + jnp.sum(theirs, axis=0)) / members
     predicted = jnp.concatenate([mine, theirs], axis=0)
     anomalies = (predicted - mean[None, :]) / (observation_spread[None, :] * square_root_scale)
@@ -188,23 +267,10 @@
     products = jnp.dot(
         anomalies, stacked.T, precision=HIGHEST, preferred_element_type=jnp.float32
     )
-    whole, summed = reduce_over_space(products)
-    for r in range(2, strip_rows):
-        other, summed = swap(r, summed)
-        swapped.append(other)
-    mixing = solve(whole) / square_root_scale
-    revised = [
-        own_rows[r]
-        + lax.dot_general(
-            mixing,
-            jnp.concatenate([own_rows[r], swapped[r]], axis=0),
-            (((0,), (0,)), ((), ())),
-            precision=HIGHEST,
-            preferred_element_type=jnp.float32,
-        )
-        for r in range(strip_rows)
-    ]
-    return (jnp.stack(revised, axis=1), jnp.stack(rows, axis=1))
+    whole, received = reduce_over_space(products)
+    rest, _ = swap(by_row[2:], received)
+    mixing = solve(whole)
+    return (finish(mixing, params, first, second, rest), predicted_state)
 
 
 def solution(mesh):

time: 162 us -> 165 us (1.019)
  Pallas kernels: 13.7 us -> 25.6 us
  waiting for transfers between devices: 26.2 us -> 35.7 us
  local copies, waits for them, and re-layouts: 19.9 us -> 11.1 us
  matrix products: 7.92 us -> 1.29 us
    pallas_call x0 -> x3, Pallas kernels: none -> 11.9 us  [the longest x1 6.62 us: finish(): pl.pallas_call(finish_kernel, grid=(PARTS,), out_shape=jax.ShapeDtypeStru...]
    ppermute x4 -> x3, waiting for transfers between devices: 19 us -> 27.6 us  [swap(): return (lax.ppermute(piece, 'member', SWAP), after)]
    unnamed x37 -> x38, local copies, waits for them, and re-layouts: 11.6 us -> 4.02 us
    dot_general x4 -> x0, matrix products: 6.64 us -> none  [strip(): lax.dot_general(mixing, jnp.concatenate([own_rows[r], swapped[r]], axis=0...]
    add x4, other arithmetic: 5.42 us -> 7.85 us  [advance(): return center + rate * flow]
    another operation x2 -> x0, other arithmetic: 1.93 us -> none  [strip(): return (jnp.stack(revised, axis=1), jnp.stack(rows, axis=1))]
    ppermute x4 -> x3, starting transfers between devices: 4.14 us -> 2.96 us  [swap(): return (lax.ppermute(piece, 'member', SWAP), after)]
  transfers between devices with their start and end apart: 11 -> 10, of which waited for: 6 -> 6; matrix products, arithmetic and copies ran while one was open for 12% -> 6% of each run, Pallas kernels for 9% -> 10%
where the time goes in v4:
time: 165 us; the launch traced here: 164 us
  blocking collectives  49.2 us (30%)
  waiting for transfers between devices  35.7 us (22%)
  starting transfers between devices  29.1 us (18%)
  Pallas kernels  25.6 us (16%)
  local copies, waits for them, and re-layouts  11.1 us (7%)
  other arithmetic  11.1 us (7%)
    all_to_all x1, blocking collectives, reduce_over_space(): pieces = lax.all_to_all(part, CHIPS, 0, 0, tiled=True)  31.6 us
    ppermute x3, waiting for transfers between devices, swap(): return (lax.ppermute(piece, 'member', SWAP), after)  27.6 us
    all_to_all x1, blocking collectives, reduce_over_space(): summed = lax.all_to_all(spread, CHIPS, 0, 0, tiled=True)  17.6 us
    ppermute x2, starting transfers between devices, halo(): above = lax.ppermute(tail, SPACE, [(i, i + 1) for i in range(ends)])  15.3 us
    pallas_call x1, Pallas kernels, solve(): pl.pallas_call(solve_kernel, out_shape=jax.ShapeDtypeStruct((m, wide - m)...  13.7 us
    add x4, other arithmetic, advance(): return center + rate * flow  7.85 us
    ppermute x1, starting transfers between devices, reduce_over_space(): part = kept + lax.ppermute(sent, 'core', SWAP)  7.22 us
    pallas_call x1, Pallas kernels, finish(): pl.pallas_call(finish_kernel, grid=(PARTS,), out_shape=jax.ShapeDtypeStru...  6.62 us
  transfers between devices with their start and end apart: 10, of which 6 were waited for; matrix products, arithmetic and copies ran while one was open for 6% of the time, Pallas kernels for 10%

profile of v4, /device:TPU:2, one launch (start us, length us, event | category | flops | bytes accessed | tf_op | source)
XLA Modules:
  0.0 164.2 jit_solution(13267371525829318684)
XLA Ops:
  0.6 2.6 %split_rows.1 = (f32[128,1024]{1,0:T(8,128)}, f32[128,1024]{1,0:T(8,128)}, f32[128,1024]{1,0:T(8,128)}, f32[128,1024]{1,0:T(8,128)}) custom-call(f32[128,4,1024]{2,1,0:T(4,128)} %x_ref.1), custom_call_target="tpu_custom_call" | custom-call | bytes 4194304 | tf_op jit(solution)/shard_map/split_rows/pallas_call | solution.py:98
  3.2 1.8 %collective-permute-start = (f32[128,1024]{1,0:T(8,128)}, f32[128,1024]{1,0:T(8,128)S(1)}, u32[]{:S(2)}, u32[]{:S(2)}) collective-permute-start(f32[128,1024]{1,0:T(8,128)} %get-tuple-element.13), channel_id=1, source_target_pairs={{0,1},{1,2},{2,3},{3,4},{4,5},{5,6},{6,7},{7,8},{8,9},{9,10},{10,1... | collective-permute-start | bytes 1572872 | tf_op jit(solution)/shard_map/ppermute | solution.py:178
  5.1 1.4 collective-permute-start.1
  6.5 2.8 %copy.14 = f32[128,4,1024]{2,0,1:T(8,128)S(1)} copy(f32[128,4,1024]{2,1,0:T(4,128)} %own_ref.1) | data formatting | bytes 4194304 | tf_op args[0]
  9.6 1.5 collective-permute-done.1
  11.1 1.8 %fusion.17 = (f32[128,1024]{1,0:T(8,128)}, f32[128,1024]{1,0:T(8,128)}) fusion(f32[128,1024]{1,0:T(8,128)S(1)} %copy-done.8, f32[128,1024]{1,0:T(8,128)S(1)} %collective-permute-done.1, f32[128,1024]{1,0:T(8,128)S(1)} %copy-done.2, f32[4,128,1024]{2,1,0:T(8,128)S(1)} %bitcast.53, f32[1024]{0:T(1024)S(1)} %bitcast.85, f32[1024]{0:T(1024)S(1)} %bitcast.87, ...), kind=kLoop, calls=%fused_computation.37 | loop fusion | flops 3670016 | bytes 5275648 | tf_op jit(solution)/shard_map/add | solution.py:187
  13.0 13.5 %collective-permute-start.2 = (f32[128,1024]{1,0:T(8,128)}, f32[128,1024]{1,0:T(8,128)}, u32[]{:S(2)}, u32[]{:S(2)}) collective-permute-start(f32[128,1024]{1,0:T(8,128)} %get-tuple-element.17), channel_id=1, source_target_pairs={{0,1},{1,2},{2,3},{3,4},{4,5},{5,6},{6,7},{7,8},{8,9},{9,10},{10,1... | collective-permute-start | bytes 1572872 | tf_op jit(solution)/shard_map/ppermute | solution.py:178
  26.5 1.3 collective-permute-start.3
  27.8 2.8 %fusion.33 = (f32[128,1024]{1,0:T(8,128)S(1)}, f32[128,1024]{1,0:T(8,128)S(1)}) fusion(f32[128,1024]{1,0:T(8,128)} %get-tuple-element.16, f32[128,1024]{1,0:T(8,128)} %collective-permute-done.2, f32[1024]{0:T(1024)S(1)} %bitcast.70, f32[1024]{0:T(1024)S(1)} %bitcast.72, f32[1024]{0:T(1024)S(1)} %bitcast.74, f32[1024]{0:T(1024)S(1)} %bitcast.76, ...), kind=kLoop, calls=%fused_computation.53 | loop fusion | flops 3670016 | bytes 4751360 | tf_op jit(solution)/shard_map/add | solution.py:187
  30.6 0.9 fusion.49
  31.5 2.4 %fusion.57 = (f32[128,1024]{1,0:T(8,128)S(1)}, f32[128,1024]{1,0:T(8,128)S(1)}) fusion(f32[128,1024]{1,0:T(8,128)S(1)} %get-tuple-element.25, f32[128,1024]{1,0:T(8,128)} %get-tuple-element.17, f32[128,1024]{1,0:T(8,128)S(1)} %get-tuple-element.23, f32[4,128,1024]{2,1,0:T(8,128)S(1)} %bitcast.56, f32[1024]{0:T(1024)S(1)} %bitcast.80, f32[1024]{0:T(1024)S(1)} %bitcast.82, ...), kind=kLoop, calls=%fused_computation.77 | loop fusion | flops 3670016 | bytes 4227072 | tf_op jit(solution)/shard_map/add | solution.py:187
  33.9 1.6 pad_maximum_fusion
  35.6 2.9 %copy.11 = f32[128,4096]{0,1:T(8,128)} copy(f32[128,4096]{1,0:T(8,128)} %pad_maximum_fusion) | data formatting | bytes 4194304 | tf_op jit(solution)/shard_map/concatenate | solution.py:255
  38.5 2.7 %gather_fusion = f32[512,128]{1,0:T(8,128)S(1)} fusion(f32[128,4096]{0,1:T(8,128)} %copy.11, s32[1024]{0:T(1024)S(1)} %pad_clamp_fusion), kind=kCustom, calls=%fused_computation | custom fusion | bytes 526336 | tf_op jit(solution)/shard_map/jit(_take)/gather | solution.py:255
  41.7 1.1 slice_bitcast_fusion.1
  43.4 4.2 %collective-permute-done.4 = f32[128,512]{0,1:T(8,128)S(1)} collective-permute-done((f32[128,512]{0,1:T(8,128)S(1)}, f32[128,512]{0,1:T(8,128)S(1)}, u32[]{:S(2)}, u32[]{:S(2)}) %collective-permute-start.4) | collective-permute-done | bytes 262176 | tf_op jit(solution)/shard_map/ppermute | solution.py:258
  48.0 1.1 fusion
  49.1 7.2 %collective-permute-start.5 = (f32[128,384]{1,0:T(8,128)S(1)}, f32[128,384]{1,0:T(8,128)S(1)}, u32[]{:S(2)}, u32[]{:S(2)}) collective-permute-start(f32[128,384]{1,0:T(8,128)S(1)} %slice_select_fusion), channel_id=1, source_target_pairs={{0,1},{1,0},{2,3},{3,2},{4,5},{5,4},{6,7},{7,6},{8,9},{9,8},{10,11... | collective-permute-start | bytes 589832 | tf_op jit(solution)/shard_map/ppermute | solution.py:215
  56.3 1.1 collective-permute-done.5
  57.5 31.6 %all_to_all.18 = f32[64,2,384]{2,1,0:T(2,128)S(1)} all-to-all(f32[64,2,384]{2,1,0:T(2,128)S(1)} %all_to_all.12), channel_id=1, replica_groups=mesh['member'=2,'z'=8,'y'=4,'xh'=2,'core'=2] {'z','y','xh'}, dimensions={0} | all-to-all | bytes 393216 | tf_op jit(solution)/shard_map/all_to_all | solution.py:217
  89.3 17.6 %all_to_all.19 = f32[64,2,384]{2,1,0:T(2,128)S(1)} all-to-all(f32[64,2,384]{2,1,0:T(2,128)S(1)} %broadcast_in_dim.7), channel_id=1, replica_groups=mesh['member'=2,'z'=8,'y'=4,'xh'=2,'core'=2] {'z','y','xh'}, dimensions={0} | all-to-all | bytes 393216 | tf_op jit(solution)/shard_map/all_to_all | solution.py:220
  107.4 1.4 collective-permute-done.6
  108.8 0.9 collective-permute-start.9
  109.7 1.1 collective-permute-start.7
  110.8 0.9 collective-permute-start.8
  111.7 2.7 %merge_rows.1 = f32[128,4,1024]{2,1,0:T(4,128)} custom-call(f32[128,1024]{1,0:T(8,128)} %copy-done.4, f32[128,1024]{1,0:T(8,128)} %copy-done.5, f32[128,1024]{1,0:T(8,128)} %copy-done.6, f32[128,1024]{1,0:T(8,128)} %copy-done.7), custom_call_target="tpu_custom_call" | custom-call | bytes 4194304 | tf_op jit(solution)/shard_map/merge_rows/pallas_call | solution.py:117
  114.5 0.8 pad_maximum_fusion.1.g_ref
  115.2 13.7 %solve.1.mix_ref = f32[256,128]{1,0:T(8,128)} custom-call(f32[256,384]{1,0:T(8,128)} %pad_maximum_fusion.1.g_ref), custom_call_target="tpu_custom_call" | custom-call | flops 200000000 | bytes 600000 | tf_op jit(solution)/shard_map/solve/pallas_call | solution.py:80
  128.9 17.1 %collective-permute-done.7.first_ref = f32[128,1024]{1,0:T(8,128)S(1)} collective-permute-done((f32[128,1024]{1,0:T(8,128)}, f32[128,1024]{1,0:T(8,128)S(1)}, u32[]{:S(2)}, u32[]{:S(2)}) %collective-permute-start.7) | collective-permute-done | bytes 524320 | tf_op jit(solution)/shard_map/ppermute | solution.py:252
  146.0 10.5 %collective-permute-done.8.second_ref = f32[128,1024]{1,0:T(8,128)} collective-permute-done((f32[128,1024]{1,0:T(8,128)}, f32[128,1024]{1,0:T(8,128)}, u32[]{:S(2)}, u32[]{:S(2)}) %collective-permute-start.8) | collective-permute-done | bytes 524320 | tf_op jit(solution)/shard_map/ppermute | solution.py:252
  156.5 1.0 copy-done.11
  157.6 6.6 %finish.1 = f32[128,4,1024]{2,1,0:T(4,128)} custom-call(f32[256,128]{1,0:T(8,128)} %solve.1.mix_ref, f32[128,4,1024]{2,1,0:T(4,128)} %own_ref.1, f32[128,1024]{1,0:T(8,128)} %copy-done.12, f32[128,1024]{1,0:T(8,128)} %collective-permute-done.8.second_ref, f32[2,128,1024]{2,1,0:T(8,128)} %copy-done.11), custom_call_target="tpu_custom_call" | custom-call | flops 268435456 | bytes 6291456 | tf_op jit(solution)/shard_map/finish/pallas_call | solution.py:151
  (59 shorter events, 2.6 us)
Async XLA Ops:
  0.6 8.7 %copy-start = (f32[8,4]{0,1:T(4,128)S(1)}, f32[8,4]{0,1:T(4,128)}, u32[]{:S(2)}) copy-start(f32[8,4]{0,1:T(4,128)} %param.11) | copy-start | bytes 388
  3.2 6.3 %collective-permute-start = (f32[128,1024]{1,0:T(8,128)}, f32[128,1024]{1,0:T(8,128)S(1)}, u32[]{:S(2)}, u32[]{:S(2)}) collective-permute-start(f32[128,1024]{1,0:T(8,128)} %get-tuple-element.13), channel_id=1, source_target_pairs={{0,1},{1,2},{2,3},{3,4},{4,5},{5,6},{6,7},{7,8},{8,9},{9,10},{10,1... | collective-permute-start | bytes 1572872 | tf_op jit(solution)/shard_map/ppermute | solution.py:178
  5.0 4.3 %copy-start.14 = (s32[4,1024]{1,0:T(4,128)S(1)}, s32[4,1024]{1,0:T(4,128)}, u32[]{:S(2)}) copy-start(s32[4,1024]{1,0:T(4,128)} %param.10) | copy-start | bytes 49156
  5.0 6.1 %copy-start.1 = (f32[128,1024]{1,0:T(8,128)S(1)}, f32[128,1024]{1,0:T(8,128)}, u32[]{:S(2)}) copy-start(f32[128,1024]{1,0:T(8,128)} %get-tuple-element.14) | copy-start | bytes 1572868
  5.0 6.1 %copy-start.2 = (f32[128,1024]{1,0:T(8,128)S(1)}, f32[128,1024]{1,0:T(8,128)}, u32[]{:S(2)}) copy-start(f32[128,1024]{1,0:T(8,128)} %get-tuple-element.15) | copy-start | bytes 1572868
  5.0 6.1 %copy-start.8 = (f32[128,1024]{1,0:T(8,128)S(1)}, f32[128,1024]{1,0:T(8,128)}, u32[]{:S(2)}) copy-start(f32[128,1024]{1,0:T(8,128)} %get-tuple-element.13) | copy-start | bytes 1572868
  5.0 6.0 %copy-start.10 = (f32[128,1024]{1,0:T(8,128)S(1)}, f32[128,1024]{1,0:T(8,128)}, u32[]{:S(2)}) copy-start(f32[128,1024]{1,0:T(8,128)} %get-tuple-element.12) | copy-start | bytes 1572868
  5.1 6.0 %collective-permute-start.1 = (f32[128,1024]{1,0:T(8,128)}, f32[128,1024]{1,0:T(8,128)S(1)}, u32[]{:S(2)}, u32[]{:S(2)}) collective-permute-start(f32[128,1024]{1,0:T(8,128)} %get-tuple-element.12), channel_id=1, source_target_pairs={{1,0},{2,1},{3,2},{4,3},{5,4},{6,5},{7,6},{8,7},{9,8},{10,9},{11,1... | collective-permute-start | bytes 1572872 | tf_op jit(solution)/shard_map/ppermute | solution.py:179
  11.1 15.4 %copy-start.17 = (s32[512]{0:T(512)S(1)}, s32[512]{0:T(512)}, u32[]{:S(2)}) copy-start(s32[512]{0:T(512)} %param.12) | copy-start | bytes 6148
  13.0 14.8 %collective-permute-start.2 = (f32[128,1024]{1,0:T(8,128)}, f32[128,1024]{1,0:T(8,128)}, u32[]{:S(2)}, u32[]{:S(2)}) collective-permute-start(f32[128,1024]{1,0:T(8,128)} %get-tuple-element.17), channel_id=1, source_target_pairs={{0,1},{1,2},{2,3},{3,4},{4,5},{5,6},{6,7},{7,8},{8,9},{9,10},{10,1... | collective-permute-start | bytes 1572872 | tf_op jit(solution)/shard_map/ppermute | solution.py:178
  26.5 5.0 %collective-permute-start.3 = (f32[128,1024]{1,0:T(8,128)}, f32[128,1024]{1,0:T(8,128)S(1)}, u32[]{:S(2)}, u32[]{:S(2)}) collective-permute-start(f32[128,1024]{1,0:T(8,128)} %get-tuple-element.16), channel_id=1, source_target_pairs={{1,0},{2,1},{3,2},{4,3},{5,4},{6,5},{7,6},{8,7},{9,8},{10,9},{11,1... | collective-permute-start | bytes 1572872 | tf_op jit(solution)/shard_map/ppermute | solution.py:179
  27.8 2.8 %copy-start.3 = (f32[128,1024]{1,0:T(8,128)S(1)}, f32[128,1024]{1,0:T(8,128)}, u32[]{:S(2)}) copy-start(f32[128,1024]{1,0:T(8,128)} %get-tuple-element.16) | copy-start | bytes 1572868
  27.8 2.8 %copy-start.9 = (f32[128,1024]{1,0:T(8,128)S(1)}, f32[128,1024]{1,0:T(8,128)}, u32[]{:S(2)}) copy-start(f32[128,1024]{1,0:T(8,128)} %get-tuple-element.13) | copy-start | bytes 1572868
  30.6 3.3 %copy-start.4 = (f32[128,1024]{1,0:T(8,128)}, f32[128,1024]{1,0:T(8,128)S(1)}, u32[]{:S(2)}) copy-start(f32[128,1024]{1,0:T(8,128)S(1)} %get-tuple-element.22.refs_0_) | copy-start | bytes 1572868
  31.5 2.4 %copy-start.5 = (f32[128,1024]{1,0:T(8,128)}, f32[128,1024]{1,0:T(8,128)S(1)}, u32[]{:S(2)}) copy-start(f32[128,1024]{1,0:T(8,128)S(1)} %get-tuple-element.24.refs_1_) | copy-start | bytes 1572868
  33.9 1.7 %copy-start.6 = (f32[128,1024]{1,0:T(8,128)}, f32[128,1024]{1,0:T(8,128)S(1)}, u32[]{:S(2)}) copy-start(f32[128,1024]{1,0:T(8,128)S(1)} %get-tuple-element.26.refs_2_) | copy-start | bytes 1572868
  33.9 1.7 %copy-start.7 = (f32[128,1024]{1,0:T(8,128)}, f32[128,1024]{1,0:T(8,128)S(1)}, u32[]{:S(2)}) copy-start(f32[128,1024]{1,0:T(8,128)S(1)} %get-tuple-element.27.refs_3_) | copy-start | bytes 1572868
  38.5 4.4 %copy-start.13 = (f32[128,512]{1,0:T(8,128)S(1)}, f32[128,512]{1,0:T(8,128)}, u32[]{:S(2)}) copy-start(f32[128,512]{1,0:T(8,128)} %param.15) | copy-start | bytes 786436
  38.5 4.7 %copy-start.15 = (f32[512]{0:T(512)S(1)}, f32[512]{0:T(512)}, u32[]{:S(2)}) copy-start(f32[512]{0:T(512)} %param.14) | copy-start | bytes 6148
  38.5 4.7 %copy-start.16 = (f32[512]{0:T(512)S(1)}, f32[512]{0:T(512)}, u32[]{:S(2)}) copy-start(f32[512]{0:T(512)} %param.13) | copy-start | bytes 6148
  41.1 6.5 %collective-permute-start.4 = (f32[128,512]{0,1:T(8,128)S(1)}, f32[128,512]{0,1:T(8,128)S(1)}, u32[]{:S(2)}, u32[]{:S(2)}) collective-permute-start(f32[128,512]{0,1:T(8,128)S(1)} %bitcast.59), channel_id=1, source_target_pairs={{0,128},{128,0},{1,129},{129,1},{2,130},{130,2},{3,131},{131,3},{4... | collective-permute-start | bytes 786440 | tf_op jit(solution)/shard_map/ppermute | solution.py:258
  49.1 8.3 %collective-permute-start.5 = (f32[128,384]{1,0:T(8,128)S(1)}, f32[128,384]{1,0:T(8,128)S(1)}, u32[]{:S(2)}, u32[]{:S(2)}) collective-permute-start(f32[128,384]{1,0:T(8,128)S(1)} %slice_select_fusion), channel_id=1, source_target_pairs={{0,1},{1,0},{2,3},{3,2},{4,5},{5,4},{6,7},{7,6},{8,9},{9,8},{10,11... | collective-permute-start | bytes 589832 | tf_op jit(solution)/shard_map/ppermute | solution.py:215
  107.0 1.7 %collective-permute-start.6 = (f32[128,384]{1,0:T(8,128)S(1)}, f32[128,384]{1,0:T(8,128)S(1)}, u32[]{:S(2)}, u32[]{:S(2)}) collective-permute-start(f32[128,384]{1,0:T(8,128)S(1)} %all_to_all.15), channel_id=1, source_target_pairs={{0,1},{1,0},{2,3},{3,2},{4,5},{5,4},{6,7},{7,6},{8,9},{9,8},{10,11... | collective-permute-start | bytes 589832 | tf_op jit(solution)/shard_map/ppermute | solution.py:221
  108.8 47.8 %collective-permute-start.9 = (f32[2,128,1024]{2,1,0:T(8,128)S(1)}, f32[2,128,1024]{2,1,0:T(8,128)S(1)}, u32[]{:S(2)}, u32[]{:S(2)}) collective-permute-start(f32[2,128,1024]{2,1,0:T(8,128)S(1)} %slice.232), channel_id=1, source_target_pairs={{0,128},{128,0},{1,129},{129,1},{2,130},{130,2},{3,131},{131,3},{4... | collective-permute-start | bytes 3145736 | tf_op jit(solution)/shard_map/ppermute | solution.py:252
  109.7 36.3 %collective-permute-start.7 = (f32[128,1024]{1,0:T(8,128)}, f32[128,1024]{1,0:T(8,128)S(1)}, u32[]{:S(2)}, u32[]{:S(2)}) collective-permute-start(f32[128,1024]{1,0:T(8,128)} %get-tuple-element.19), channel_id=1, source_target_pairs={{0,128},{128,0},{1,129},{129,1},{2,130},{130,2},{3,131},{131,3},{4... | collective-permute-start | bytes 1572872 | tf_op jit(solution)/shard_map/ppermute | solution.py:252
  110.8 45.8 %collective-permute-start.8 = (f32[128,1024]{1,0:T(8,128)}, f32[128,1024]{1,0:T(8,128)}, u32[]{:S(2)}, u32[]{:S(2)}) collective-permute-start(f32[128,1024]{1,0:T(8,128)} %get-tuple-element.20), channel_id=1, source_target_pairs={{0,128},{128,0},{1,129},{129,1},{2,130},{130,2},{3,131},{131,3},{4... | collective-permute-start | bytes 1572872 | tf_op jit(solution)/shard_map/ppermute | solution.py:252
  146.0 10.5 %copy-start.12 = (f32[128,1024]{1,0:T(8,128)}, f32[128,1024]{1,0:T(8,128)S(1)}, u32[]{:S(2)}) copy-start(f32[128,1024]{1,0:T(8,128)S(1)} %collective-permute-done.7.first_ref) | copy-start | bytes 1572868
  156.5 1.0 copy-start.11

commit v5 on v4

--- a/solution.py
+++ b/solution.py
@@ -127,14 +127,19 @@
     )(*rows)
 
 
-def finish_kernel(mix_ref, own_ref, first_ref, second_ref, rest_ref, out_ref):
+def finish_kernel(mix_ref, own_ref, first_ref, middle_ref, last_ref, out_ref):
     m, rows, _ = own_ref.shape
     dims = (((0,), (0,)), ((), ()))
     mix = mix_ref[...] * (1.0 / math.sqrt(2 * m - 1))
     low, high = mix[:m, :], mix[m:, :]
     for r in range(rows):
         mine = own_ref[:, r, :]
-        other = (first_ref, second_ref)[r][...] if r < 2 else rest_ref[r - 2]
+        if r == 0:
+            other = first_ref[...]
+        elif r == rows - 1:
+            other = last_ref[...]
+        else:
+            other = middle_ref[r - 1]
         out_ref[:, r, :] = mine + (
             lax.dot_general(low, mine, dims, precision=HIGHEST, preferred_element_type=jnp.float32)
             + lax.dot_general(
@@ -143,7 +148,7 @@
         )
 
 
-def finish(mixing, params, first, second, rest):
+def finish(mixing, params, first, middle, last):
     m, rows, cols = params.shape
     piece = cols // PARTS
     flat = pl.BlockSpec((m, piece), lambda i: (0, i))
@@ -156,15 +161,15 @@
             pl.BlockSpec((2 * m, m), lambda i: (0, 0)),
             whole,
             flat,
+            pl.BlockSpec((rows - 2, m, piece), lambda i: (0, 0, i)),
             flat,
-            pl.BlockSpec((rows - 2, m, piece), lambda i: (0, 0, i)),
         ],
         out_specs=whole,
         cost_estimate=pl.CostEstimate(
             flops=4 * m * m * rows * cols, bytes_accessed=12 * params.size, transcendentals=0
         ),
         name="finish",
-    )(mixing, params, first, second, rest)
+    )(mixing, params, first, middle, last)
 
 
 def coef_fields(regime, regime_coefs):
@@ -256,7 +261,7 @@
     first, _ = swap(own_rows[0], edge)
     predicted_state = merge_rows(rows)
     theirs = lax.ppermute(mine, "member", SWAP)
-    second, theirs = swap(own_rows[1], theirs)
+    middle, theirs = swap(by_row[1:3], theirs)
     mean = (jnp.sum(mine, axis=0) + jnp.sum(theirs, axis=0)) / members
     predicted = jnp.concatenate([mine, theirs], axis=0)
     anomalies = (predicted - mean[None, :]) / (observation_spread[None, :] * square_root_scale)
@@ -268,9 +273,9 @@
         anomalies, stacked.T, precision=HIGHEST, preferred_element_type=jnp.float32
     )
     whole, received = reduce_over_space(products)
-    rest, _ = swap(by_row[2:], received)
+    last, _ = swap(own_rows[3], received)
     mixing = solve(whole)
-    return (finish(mixing, params, first, second, rest), predicted_state)
+    return (finish(mixing, params, first, middle, last), predicted_state)
 
 
 def solution(mesh):

time: 165 us -> 154 us (0.933)
  blocking collectives: 49.2 us -> 31.6 us
  starting transfers between devices: 29.1 us -> 33.8 us
  local copies, waits for them, and re-layouts: 11.1 us -> 13.1 us
  waiting for transfers between devices: 35.7 us -> 34 us
    all_to_all x1 -> x0, blocking collectives: 17.6 us -> none  [reduce_over_space(): summed = lax.all_to_all(spread, CHIPS, 0, 0, tiled=True)]
    ppermute x3, waiting for transfers between devices: 27.6 us -> 15.2 us  [swap(): return (lax.ppermute(piece, 'member', SWAP), after)]
    all_to_all x0 -> x1, waiting for transfers between devices: none -> 12 us  [reduce_over_space(): summed = lax.all_to_all(spread, CHIPS, 0, 0, tiled=True)]
    all_to_all x0 -> x1, starting transfers between devices: none -> 4.73 us  [reduce_over_space(): summed = lax.all_to_all(spread, CHIPS, 0, 0, tiled=True)]
    unnamed x38 -> x42, local copies, waits for them, and re-layouts: 4.02 us -> 4.37 us
  transfers between devices with their start and end apart: 10 -> 11, of which waited for: 6 -> 6; matrix products, arithmetic and copies ran while one was open for 6% -> 7% of each run, Pallas kernels for 10% -> 11%
where the time goes in v5:
time: 154 us; the launch traced here: 153 us
  waiting for transfers between devices  34 us (22%)
  starting transfers between devices  33.8 us (22%)
  blocking collectives  31.6 us (21%)
  Pallas kernels  26 us (17%)
  local copies, waits for them, and re-layouts  13.1 us (9%)
  other arithmetic  12.1 us (8%)
    all_to_all x1, blocking collectives, reduce_over_space(): pieces = lax.all_to_all(part, CHIPS, 0, 0, tiled=True)  31.6 us
    ppermute x2, starting transfers between devices, halo(): above = lax.ppermute(tail, SPACE, [(i, i + 1) for i in range(ends)])  15.3 us
    ppermute x3, waiting for transfers between devices, swap(): return (lax.ppermute(piece, 'member', SWAP), after)  15.2 us
    pallas_call x1, Pallas kernels, solve(): pl.pallas_call(solve_kernel, out_shape=jax.ShapeDtypeStruct((m, wide - m)...  13.7 us
    all_to_all x1, waiting for transfers between devices, reduce_over_space(): summed = lax.all_to_all(spread, CHIPS, 0, 0, tiled=True)  12 us
    add x4, other arithmetic, advance(): return center + rate * flow  7.89 us
    ppermute x1, starting transfers between devices, reduce_over_space(): part = kept + lax.ppermute(sent, 'core', SWAP)  7.19 us
    pallas_call x1, Pallas kernels, finish(): pl.pallas_call(finish_kernel, grid=(PARTS,), out_shape=jax.ShapeDtypeStru...  6.94 us
  transfers between devices with their start and end apart: 11, of which 6 were waited for; matrix products, arithmetic and copies ran while one was open for 7% of the time, Pallas kernels for 11%

profile of v5, /device:TPU:2, one launch (start us, length us, event | category | flops | bytes accessed | tf_op | source)
XLA Modules:
  0.0 153.0 jit_solution(13790291710971650623)
XLA Ops:
  0.6 2.6 %split_rows.1 = (f32[128,1024]{1,0:T(8,128)}, f32[128,1024]{1,0:T(8,128)}, f32[128,1024]{1,0:T(8,128)}, f32[128,1024]{1,0:T(8,128)}) custom-call(f32[128,4,1024]{2,1,0:T(4,128)} %x_ref.1), custom_call_target="tpu_custom_call" | custom-call | bytes 4194304 | tf_op jit(solution)/shard_map/split_rows/pallas_call | solution.py:98
  3.2 1.8 %collective-permute-start = (f32[128,1024]{1,0:T(8,128)}, f32[128,1024]{1,0:T(8,128)S(1)}, u32[]{:S(2)}, u32[]{:S(2)}) collective-permute-start(f32[128,1024]{1,0:T(8,128)} %get-tuple-element.13), channel_id=1, source_target_pairs={{0,1},{1,2},{2,3},{3,4},{4,5},{5,6},{6,7},{7,8},{8,9},{9,10},{10,1... | collective-permute-start | bytes 1572872 | tf_op jit(solution)/shard_map/ppermute | solution.py:183
  5.1 1.4 collective-permute-start.1
  6.5 2.8 %copy.14 = f32[128,4,1024]{2,0,1:T(8,128)S(1)} copy(f32[128,4,1024]{2,1,0:T(4,128)} %own_ref.1) | data formatting | bytes 4194304 | tf_op args[0]
  9.6 1.5 collective-permute-done.1
  11.1 1.8 %fusion.17 = (f32[128,1024]{1,0:T(8,128)}, f32[128,1024]{1,0:T(8,128)}) fusion(f32[128,1024]{1,0:T(8,128)S(1)} %copy-done.8, f32[128,1024]{1,0:T(8,128)S(1)} %collective-permute-done.1, f32[128,1024]{1,0:T(8,128)S(1)} %copy-done.2, f32[1024]{0:T(1024)S(1)} %bitcast.85, f32[1024]{0:T(1024)S(1)} %bitcast.87, f32[1024]{0:T(1024)S(1)} %bitcast.89, ...), kind=kLoop, calls=%fused_computation.37 | loop fusion | flops 3670016 | bytes 5275648 | tf_op jit(solution)/shard_map/add | solution.py:192
  13.0 13.5 %collective-permute-start.2 = (f32[128,1024]{1,0:T(8,128)}, f32[128,1024]{1,0:T(8,128)}, u32[]{:S(2)}, u32[]{:S(2)}) collective-permute-start(f32[128,1024]{1,0:T(8,128)} %get-tuple-element.17), channel_id=1, source_target_pairs={{0,1},{1,2},{2,3},{3,4},{4,5},{5,6},{6,7},{7,8},{8,9},{9,10},{10,1... | collective-permute-start | bytes 1572872 | tf_op jit(solution)/shard_map/ppermute | solution.py:183
  26.5 1.3 collective-permute-start.3
  27.8 2.8 %fusion.33 = (f32[128,1024]{1,0:T(8,128)S(1)}, f32[128,1024]{1,0:T(8,128)S(1)}) fusion(f32[128,1024]{1,0:T(8,128)} %get-tuple-element.16, f32[128,1024]{1,0:T(8,128)} %collective-permute-done.2, f32[1024]{0:T(1024)S(1)} %bitcast.70, f32[1024]{0:T(1024)S(1)} %bitcast.72, f32[1024]{0:T(1024)S(1)} %bitcast.74, f32[1024]{0:T(1024)S(1)} %bitcast.76, ...), kind=kLoop, calls=%fused_computation.53 | loop fusion | flops 3670016 | bytes 4751360 | tf_op jit(solution)/shard_map/add | solution.py:192
  30.7 0.9 fusion.49
  31.6 2.4 %fusion.57 = (f32[128,1024]{1,0:T(8,128)S(1)}, f32[128,1024]{1,0:T(8,128)S(1)}) fusion(f32[128,1024]{1,0:T(8,128)S(1)} %get-tuple-element.25, f32[128,1024]{1,0:T(8,128)} %get-tuple-element.17, f32[128,1024]{1,0:T(8,128)S(1)} %get-tuple-element.23, f32[4,128,1024]{2,1,0:T(8,128)S(1)} %bitcast.56, f32[1024]{0:T(1024)S(1)} %bitcast.80, f32[1024]{0:T(1024)S(1)} %bitcast.82, ...), kind=kLoop, calls=%fused_computation.77 | loop fusion | flops 3670016 | bytes 4227072 | tf_op jit(solution)/shard_map/add | solution.py:192
  34.0 1.6 %pad_maximum_fusion = f32[128,4096]{1,0:T(8,128)} fusion(f32[128,1024]{1,0:T(8,128)S(1)} %get-tuple-element.27.refs_3_, f32[128,1024]{1,0:T(8,128)S(1)} %get-tuple-element.26.refs_2_, f32[128,1024]{1,0:T(8,128)S(1)} %get-tuple-element.24.refs_1_, f32[128,1024]{1,0:T(8,128)S(1)} %get-tuple-element.22.refs_0_), kind=kLoop, calls=%fused_computation.1 | loop fusion | flops 1572864 | bytes 4194304 | tf_op jit(solution)/shard_map/concatenate | solution.py:260
  35.6 2.9 %copy.11 = f32[128,4096]{0,1:T(8,128)} copy(f32[128,4096]{1,0:T(8,128)} %pad_maximum_fusion) | data formatting | bytes 4194304 | tf_op jit(solution)/shard_map/concatenate | solution.py:260
  38.5 2.7 %gather_fusion = f32[512,128]{1,0:T(8,128)S(1)} fusion(f32[128,4096]{0,1:T(8,128)} %copy.11, s32[1024]{0:T(1024)S(1)} %pad_clamp_fusion), kind=kCustom, calls=%fused_computation | custom fusion | bytes 526336 | tf_op jit(solution)/shard_map/jit(_take)/gather | solution.py:260
  41.8 1.1 slice.230
  43.4 4.2 %collective-permute-done.4 = f32[128,512]{0,1:T(8,128)S(1)} collective-permute-done((f32[128,512]{0,1:T(8,128)S(1)}, f32[128,512]{0,1:T(8,128)S(1)}, u32[]{:S(2)}, u32[]{:S(2)}) %collective-permute-start.4) | collective-permute-done | bytes 262176 | tf_op jit(solution)/shard_map/ppermute | solution.py:263
  48.3 1.2 fusion.72
  49.5 1.1 fusion
  50.6 7.2 %collective-permute-start.5 = (f32[128,384]{1,0:T(8,128)S(1)}, f32[128,384]{1,0:T(8,128)S(1)}, u32[]{:S(2)}, u32[]{:S(2)}) collective-permute-start(f32[128,384]{1,0:T(8,128)S(1)} %slice_select_fusion), channel_id=1, source_target_pairs={{0,1},{1,0},{2,3},{3,2},{4,5},{5,4},{6,7},{7,6},{8,9},{9,8},{10,11... | collective-permute-start | bytes 589832 | tf_op jit(solution)/shard_map/ppermute | solution.py:220
  57.8 1.1 collective-permute-done.5
  59.0 31.6 %all_to_all.18 = f32[64,2,384]{2,1,0:T(2,128)S(1)} all-to-all(f32[64,2,384]{2,1,0:T(2,128)S(1)} %all_to_all.12), channel_id=1, replica_groups=mesh['member'=2,'z'=8,'y'=4,'xh'=2,'core'=2] {'z','y','xh'}, dimensions={0} | all-to-all | bytes 393216 | tf_op jit(solution)/shard_map/all_to_all | solution.py:222
  91.5 4.7 %all-to-all-start.1 = ((f32[64,2,384]{2,1,0:T(2,128)}), f32[64,2,384]{2,1,0:T(2,128)S(1)}, u32[]{:S(2)}, u32[]{:S(2)}) async-start(f32[64,2,384]{2,1,0:T(2,128)} %broadcast_in_dim.7), calls=%async_computation.1 | async-start | bytes 393216 | tf_op jit(solution)/shard_map/all_to_all | solution.py:225
  96.2 1.2 collective-permute-start.8
  97.4 12.0 %all-to-all-done.1 = f32[64,2,384]{2,1,0:T(2,128)S(1)} async-done(((f32[64,2,384]{2,1,0:T(2,128)}), f32[64,2,384]{2,1,0:T(2,128)S(1)}, u32[]{:S(2)}, u32[]{:S(2)}) %all-to-all-start.1) | async-done | bytes 196640 | tf_op jit(solution)/shard_map/all_to_all | solution.py:225
  109.6 1.1 slice_bitcast_fusion
  110.7 0.9 collective-permute-start.7
  111.6 1.2 collective-permute-start.9
  112.7 2.7 %merge_rows.1 = f32[128,4,1024]{2,1,0:T(4,128)} custom-call(f32[128,1024]{1,0:T(8,128)} %copy-done.4, f32[128,1024]{1,0:T(8,128)} %copy-done.5, f32[128,1024]{1,0:T(8,128)} %copy-done.6, f32[128,1024]{1,0:T(8,128)} %copy-done.7), custom_call_target="tpu_custom_call" | custom-call | bytes 4194304 | tf_op jit(solution)/shard_map/merge_rows/pallas_call | solution.py:117
  116.3 13.7 %solve.1.mix_ref = f32[256,128]{1,0:T(8,128)} custom-call(f32[256,384]{1,0:T(8,128)} %pad_maximum_fusion.1.g_ref), custom_call_target="tpu_custom_call" | custom-call | flops 200000000 | bytes 600000 | tf_op jit(solution)/shard_map/solve/pallas_call | solution.py:80
  130.0 5.2 %collective-permute-done.7.first_ref = f32[128,1024]{1,0:T(8,128)S(1)} collective-permute-done((f32[128,1024]{1,0:T(8,128)}, f32[128,1024]{1,0:T(8,128)S(1)}, u32[]{:S(2)}, u32[]{:S(2)}) %collective-permute-start.7) | collective-permute-done | bytes 524320 | tf_op jit(solution)/shard_map/ppermute | solution.py:257
  135.2 10.0 %collective-permute-done.9.last_ref = f32[128,1024]{1,0:T(8,128)S(1)} collective-permute-done((f32[128,1024]{1,0:T(8,128)}, f32[128,1024]{1,0:T(8,128)S(1)}, u32[]{:S(2)}, u32[]{:S(2)}) %collective-permute-start.9) | collective-permute-done | bytes 524320 | tf_op jit(solution)/shard_map/ppermute | solution.py:257
  146.0 6.9 %finish.1 = f32[128,4,1024]{2,1,0:T(4,128)} custom-call(f32[256,128]{1,0:T(8,128)} %solve.1.mix_ref, f32[128,4,1024]{2,1,0:T(4,128)} %own_ref.1, f32[128,1024]{1,0:T(8,128)} %copy-done.13, f32[2,128,1024]{2,1,0:T(8,128)} %copy-done.11, f32[128,1024]{1,0:T(8,128)} %copy-done.14), custom_call_target="tpu_custom_call" | custom-call | flops 268435456 | bytes 6291456 | tf_op jit(solution)/shard_map/finish/pallas_call | solution.py:156
  (64 shorter events, 5.0 us)
Async XLA Ops:
  0.6 8.7 %copy-start = (f32[8,4]{0,1:T(4,128)S(1)}, f32[8,4]{0,1:T(4,128)}, u32[]{:S(2)}) copy-start(f32[8,4]{0,1:T(4,128)} %param.11) | copy-start | bytes 388
  3.2 6.3 %collective-permute-start = (f32[128,1024]{1,0:T(8,128)}, f32[128,1024]{1,0:T(8,128)S(1)}, u32[]{:S(2)}, u32[]{:S(2)}) collective-permute-start(f32[128,1024]{1,0:T(8,128)} %get-tuple-element.13), channel_id=1, source_target_pairs={{0,1},{1,2},{2,3},{3,4},{4,5},{5,6},{6,7},{7,8},{8,9},{9,10},{10,1... | collective-permute-start | bytes 1572872 | tf_op jit(solution)/shard_map/ppermute | solution.py:183
  5.0 4.3 %copy-start.16 = (s32[4,1024]{1,0:T(4,128)S(1)}, s32[4,1024]{1,0:T(4,128)}, u32[]{:S(2)}) copy-start(s32[4,1024]{1,0:T(4,128)} %param.10) | copy-start | bytes 49156
  5.0 6.1 %copy-start.1 = (f32[128,1024]{1,0:T(8,128)S(1)}, f32[128,1024]{1,0:T(8,128)}, u32[]{:S(2)}) copy-start(f32[128,1024]{1,0:T(8,128)} %get-tuple-element.14) | copy-start | bytes 1572868
  5.0 6.1 %copy-start.2 = (f32[128,1024]{1,0:T(8,128)S(1)}, f32[128,1024]{1,0:T(8,128)}, u32[]{:S(2)}) copy-start(f32[128,1024]{1,0:T(8,128)} %get-tuple-element.15) | copy-start | bytes 1572868
  5.0 6.1 %copy-start.8 = (f32[128,1024]{1,0:T(8,128)S(1)}, f32[128,1024]{1,0:T(8,128)}, u32[]{:S(2)}) copy-start(f32[128,1024]{1,0:T(8,128)} %get-tuple-element.13) | copy-start | bytes 1572868
  5.1 6.0 %copy-start.10 = (f32[128,1024]{1,0:T(8,128)S(1)}, f32[128,1024]{1,0:T(8,128)}, u32[]{:S(2)}) copy-start(f32[128,1024]{1,0:T(8,128)} %get-tuple-element.12) | copy-start | bytes 1572868
  5.1 6.0 %collective-permute-start.1 = (f32[128,1024]{1,0:T(8,128)}, f32[128,1024]{1,0:T(8,128)S(1)}, u32[]{:S(2)}, u32[]{:S(2)}) collective-permute-start(f32[128,1024]{1,0:T(8,128)} %get-tuple-element.12), channel_id=1, source_target_pairs={{1,0},{2,1},{3,2},{4,3},{5,4},{6,5},{7,6},{8,7},{9,8},{10,9},{11,1... | collective-permute-start | bytes 1572872 | tf_op jit(solution)/shard_map/ppermute | solution.py:184
  11.1 15.4 %copy-start.19 = (s32[512]{0:T(512)S(1)}, s32[512]{0:T(512)}, u32[]{:S(2)}) copy-start(s32[512]{0:T(512)} %param.12) | copy-start | bytes 6148
  13.0 14.8 %collective-permute-start.2 = (f32[128,1024]{1,0:T(8,128)}, f32[128,1024]{1,0:T(8,128)}, u32[]{:S(2)}, u32[]{:S(2)}) collective-permute-start(f32[128,1024]{1,0:T(8,128)} %get-tuple-element.17), channel_id=1, source_target_pairs={{0,1},{1,2},{2,3},{3,4},{4,5},{5,6},{6,7},{7,8},{8,9},{9,10},{10,1... | collective-permute-start | bytes 1572872 | tf_op jit(solution)/shard_map/ppermute | solution.py:183
  26.5 5.0 %collective-permute-start.3 = (f32[128,1024]{1,0:T(8,128)}, f32[128,1024]{1,0:T(8,128)S(1)}, u32[]{:S(2)}, u32[]{:S(2)}) collective-permute-start(f32[128,1024]{1,0:T(8,128)} %get-tuple-element.16), channel_id=1, source_target_pairs={{1,0},{2,1},{3,2},{4,3},{5,4},{6,5},{7,6},{8,7},{9,8},{10,9},{11,1... | collective-permute-start | bytes 1572872 | tf_op jit(solution)/shard_map/ppermute | solution.py:184
  27.8 2.9 %copy-start.3 = (f32[128,1024]{1,0:T(8,128)S(1)}, f32[128,1024]{1,0:T(8,128)}, u32[]{:S(2)}) copy-start(f32[128,1024]{1,0:T(8,128)} %get-tuple-element.16) | copy-start | bytes 1572868
  27.8 2.9 %copy-start.9 = (f32[128,1024]{1,0:T(8,128)S(1)}, f32[128,1024]{1,0:T(8,128)}, u32[]{:S(2)}) copy-start(f32[128,1024]{1,0:T(8,128)} %get-tuple-element.13) | copy-start | bytes 1572868
  30.7 3.3 %copy-start.4 = (f32[128,1024]{1,0:T(8,128)}, f32[128,1024]{1,0:T(8,128)S(1)}, u32[]{:S(2)}) copy-start(f32[128,1024]{1,0:T(8,128)S(1)} %get-tuple-element.22.refs_0_) | copy-start | bytes 1572868
  31.5 2.4 %copy-start.5 = (f32[128,1024]{1,0:T(8,128)}, f32[128,1024]{1,0:T(8,128)S(1)}, u32[]{:S(2)}) copy-start(f32[128,1024]{1,0:T(8,128)S(1)} %get-tuple-element.24.refs_1_) | copy-start | bytes 1572868
  34.0 1.7 %copy-start.6 = (f32[128,1024]{1,0:T(8,128)}, f32[128,1024]{1,0:T(8,128)S(1)}, u32[]{:S(2)}) copy-start(f32[128,1024]{1,0:T(8,128)S(1)} %get-tuple-element.26.refs_2_) | copy-start | bytes 1572868
  34.0 1.7 %copy-start.7 = (f32[128,1024]{1,0:T(8,128)}, f32[128,1024]{1,0:T(8,128)S(1)}, u32[]{:S(2)}) copy-start(f32[128,1024]{1,0:T(8,128)S(1)} %get-tuple-element.27.refs_3_) | copy-start | bytes 1572868
  38.5 4.4 %copy-start.15 = (f32[128,512]{1,0:T(8,128)S(1)}, f32[128,512]{1,0:T(8,128)}, u32[]{:S(2)}) copy-start(f32[128,512]{1,0:T(8,128)} %param.15) | copy-start | bytes 786436
  38.5 4.7 %copy-start.17 = (f32[512]{0:T(512)S(1)}, f32[512]{0:T(512)}, u32[]{:S(2)}) copy-start(f32[512]{0:T(512)} %param.14) | copy-start | bytes 6148
  38.5 4.7 %copy-start.18 = (f32[512]{0:T(512)S(1)}, f32[512]{0:T(512)}, u32[]{:S(2)}) copy-start(f32[512]{0:T(512)} %param.13) | copy-start | bytes 6148
  41.2 6.5 %collective-permute-start.4 = (f32[128,512]{0,1:T(8,128)S(1)}, f32[128,512]{0,1:T(8,128)S(1)}, u32[]{:S(2)}, u32[]{:S(2)}) collective-permute-start(f32[128,512]{0,1:T(8,128)S(1)} %bitcast.59), channel_id=1, source_target_pairs={{0,128},{128,0},{1,129},{129,1},{2,130},{130,2},{3,131},{131,3},{4... | collective-permute-start | bytes 786440 | tf_op jit(solution)/shard_map/ppermute | solution.py:263
  47.6 0.7 copy-start.12
  50.6 8.3 %collective-permute-start.5 = (f32[128,384]{1,0:T(8,128)S(1)}, f32[128,384]{1,0:T(8,128)S(1)}, u32[]{:S(2)}, u32[]{:S(2)}) collective-permute-start(f32[128,384]{1,0:T(8,128)S(1)} %slice_select_fusion), channel_id=1, source_target_pairs={{0,1},{1,0},{2,3},{3,2},{4,5},{5,4},{6,7},{7,6},{8,9},{9,8},{10,11... | collective-permute-start | bytes 589832 | tf_op jit(solution)/shard_map/ppermute | solution.py:220
  91.5 17.9 %all-to-all-start.1 = ((f32[64,2,384]{2,1,0:T(2,128)}), f32[64,2,384]{2,1,0:T(2,128)S(1)}, u32[]{:S(2)}, u32[]{:S(2)}) async-start(f32[64,2,384]{2,1,0:T(2,128)} %broadcast_in_dim.7), calls=%async_computation.1 | async-start | bytes 393216 | tf_op jit(solution)/shard_map/all_to_all | solution.py:225
  96.2 39.0 %collective-permute-start.8 = (f32[2,128,1024]{2,1,0:T(8,128)}, f32[2,128,1024]{2,1,0:T(8,128)S(1)}, u32[]{:S(2)}, u32[]{:S(2)}) collective-permute-start(f32[2,128,1024]{2,1,0:T(8,128)} %slice.230), channel_id=1, source_target_pairs={{0,128},{128,0},{1,129},{129,1},{2,130},{130,2},{3,131},{131,3},{4... | collective-permute-start | bytes 3145736 | tf_op jit(solution)/shard_map/ppermute | solution.py:257
  109.5 2.1 %collective-permute-start.6 = (f32[128,384]{1,0:T(8,128)S(1)}, f32[128,384]{1,0:T(8,128)S(1)}, u32[]{:S(2)}, u32[]{:S(2)}) collective-permute-start(f32[128,384]{1,0:T(8,128)S(1)} %all_to_all.15), channel_id=1, source_target_pairs={{0,1},{1,0},{2,3},{3,2},{4,5},{5,4},{6,7},{7,6},{8,9},{9,8},{10,11... | collective-permute-start | bytes 589832 | tf_op jit(solution)/shard_map/ppermute | solution.py:226
  110.7 24.5 %collective-permute-start.7 = (f32[128,1024]{1,0:T(8,128)}, f32[128,1024]{1,0:T(8,128)S(1)}, u32[]{:S(2)}, u32[]{:S(2)}) collective-permute-start(f32[128,1024]{1,0:T(8,128)} %get-tuple-element.19), channel_id=1, source_target_pairs={{0,128},{128,0},{1,129},{129,1},{2,130},{130,2},{3,131},{131,3},{4... | collective-permute-start | bytes 1572872 | tf_op jit(solution)/shard_map/ppermute | solution.py:257
  111.6 33.6 %collective-permute-start.9 = (f32[128,1024]{1,0:T(8,128)}, f32[128,1024]{1,0:T(8,128)S(1)}, u32[]{:S(2)}, u32[]{:S(2)}) collective-permute-start(f32[128,1024]{1,0:T(8,128)} %get-tuple-element.21), channel_id=1, source_target_pairs={{0,128},{128,0},{1,129},{129,1},{2,130},{130,2},{3,131},{131,3},{4... | collective-permute-start | bytes 1572872 | tf_op jit(solution)/shard_map/ppermute | solution.py:257
  135.2 10.0 %copy-start.13 = (f32[128,1024]{1,0:T(8,128)}, f32[128,1024]{1,0:T(8,128)S(1)}, u32[]{:S(2)}) copy-start(f32[128,1024]{1,0:T(8,128)S(1)} %collective-permute-done.7.first_ref) | copy-start | bytes 1572868
  135.2 10.0 %copy-start.11 = (f32[2,128,1024]{2,1,0:T(8,128)}, f32[2,128,1024]{2,1,0:T(8,128)S(1)}, u32[]{:S(2)}) copy-start(f32[2,128,1024]{2,1,0:T(8,128)S(1)} %collective-permute-done.8.middle_ref) | copy-start | bytes 3145732
  145.2 0.8 copy-start.14
